TPU v7x, 128 devices: a whole 4x4x4 slice. The times are simulated.
128 devices in a mesh: seq: 64 (over z, y, x), exp: 2 (over core).
Axes of the slice: x: 4, y: 4, z: 4, core: 2. Of those that a mesh axis runs over, the one named last changes fastest.
Arguments:
- queries: bfloat16 [16384, 1024], P('seq', 'exp'), may hold values from -170 to 170
- keys: bfloat16 [16384, 1024], P('seq', 'exp'), may hold values from -5 to 5
- values: bfloat16 [16384, 1024], P('seq', 'exp'), may hold values from -6 to 6
- resid: bfloat16 [16384, 2048], P(('seq', 'exp')), may hold values from -6 to 6
- pair_ids: int32 [16384], replicated, may hold values from 0 to 63, never falling along the last dimension, each value on 1 to 512 neighbouring positions
- out_weight: bfloat16 [1024, 2048], P('exp'), may hold values from -0.1875 to 0.1875
- norm_gain: float32 [2048], replicated, may hold values from 0.5 to 1.5
- experts: int32 [16384, 6], P(('seq', 'exp')), may hold values from 0 to 63, all different within a row; in each aligned block of 128 rows (0 to 127, 128 to 255, ...) at most 24 rows name the same one
- gates: float32 [16384, 6], P(('seq', 'exp')), may hold values from 0.05 to 0.5
- w_gate: bfloat16 [64, 2048, 704], P('seq', None, 'exp'), may hold values from -0.125 to 0.125
- w_up: bfloat16 [64, 2048, 704], P('seq', None, 'exp'), may hold values from -0.125 to 0.125
- w_down: bfloat16 [64, 704, 2048], P('seq', 'exp'), may hold values from -0.21875 to 0.21875
Outputs:
- mixed: bfloat16 [16384, 2048], P(('seq', 'exp'))
Inputs may be any that keep to these rules, and one draw needn't show every extreme that they name: In the aligned blocks of 128 rows no expert is named more than 24 times, a bound that some block reaches; each row names 6 different experts. `pair_ids`: pair numbers never fall along the sequence; each pair has 1 to 512 tokens, one exactly that many.
All inputs are finite; a program needn't handle non-finite values.
Results may differ from a plain program's by a relative error of at most 0.012.
Values may be sent and summed in bfloat16 or wider, within the bound.
A program may use at most 128 MiB of HBM per device.

v0:
```python
import math

import jax
import jax.numpy as jnp
from jax import lax
from jax.sharding import PartitionSpec as P

HD = 128
TOP = 6


def with_halo(cells, sides, width):
    for axis, dim in sides:
        count = lax.axis_size(axis)
        ends = count - 1
        head = lax.slice_in_dim(cells, 0, width, axis=dim)
        tail = lax.slice_in_dim(cells, cells.shape[dim] - width, cells.shape[dim], axis=dim)
        cells = jnp.concatenate(
            [
                lax.ppermute(tail, axis, [(i, (i + 1) % count) for i in range(ends)]),
                cells,
                lax.ppermute(head, axis, [((i + 1) % count, i) for i in range(ends)]),
            ],
            axis=dim,
        )
    return cells


def send_back(result):
    return lax.all_to_all(result, "seq", split_axis=0, concat_axis=0, tiled=True)


def shards(
    queries,
    keys,
    values,
    resid,
    pair_ids,
    out_weight,
    norm_gain,
    experts,
    gates,
    w_gate,
    w_up,
    w_down,
):
    tok_rows = queries.shape[0]
    local_width = queries.shape[1]
    local_heads = local_width // HD
    shard = lax.axis_index("seq")
    stacked = jnp.stack([keys, values])
    widened = with_halo(stacked, (("seq", 1),), tok_rows)
    id_pad = jnp.pad(pair_ids, (tok_rows, tok_rows), constant_values=-1)
    key_ids = lax.dynamic_slice_in_dim(id_pad, shard * tok_rows, 3 * tok_rows, 0)
    query_ids = lax.dynamic_slice_in_dim(id_pad, shard * tok_rows + tok_rows, tok_rows, 0)
    query_pos = jnp.arange(tok_rows, dtype=jnp.int32) + tok_rows
    key_pos = jnp.arange(3 * tok_rows, dtype=jnp.int32)
    allowed = (query_ids[:, None] == key_ids[None, :]) & (
        jnp.abs(query_pos[:, None] - key_pos[None, :]) < tok_rows
    )
    query_heads = queries.reshape(tok_rows, local_heads, HD)
    key_heads = widened[0].reshape(3 * tok_rows, local_heads, HD)
    value_heads = widened[1].reshape(3 * tok_rows, local_heads, HD)
    score = jnp.einsum(
        "qhd,khd->hqk", query_heads, key_heads, preferred_element_type=jnp.float32
    ) / math.sqrt(HD)
    score = jnp.where(allowed[None], score, -jnp.inf)
    top = jnp.max(score, axis=-1, keepdims=True)
    weights = jnp.exp(score - top)
    probs = (weights / jnp.sum(weights, axis=-1, keepdims=True)).astype(jnp.bfloat16)
    attended = jnp.einsum("hqk,khd->qhd", probs, value_heads, preferred_element_type=jnp.float32)
    attended = attended.reshape(tok_rows, local_width).astype(jnp.bfloat16)
    moe_rows = resid.shape[0]
    projected = lax.psum(
        jnp.dot(attended, out_weight, preferred_element_type=jnp.float32).astype(jnp.bfloat16),
        "exp",
    ).astype(jnp.float32)
    projected = lax.dynamic_slice_in_dim(projected, lax.axis_index("exp") * moe_rows, moe_rows, 0)
    stream = resid.astype(jnp.float32) + projected
    meansq = jnp.mean(stream * stream, axis=-1, keepdims=True)
    normed = (stream * lax.rsqrt(meansq + 1e-05) * norm_gain).astype(jnp.bfloat16)
    n_experts = lax.axis_size("seq") * w_gate.shape[0]
    capacity = 2 * moe_rows * TOP // n_experts
    flat_experts = experts.reshape(-1)
    onehot = (flat_experts[:, None] == jnp.arange(n_experts, dtype=jnp.int32)[None, :]).astype(
        jnp.int32
    )
    ranks = jnp.cumsum(onehot, axis=0) - onehot
    slot_index = jnp.sum(ranks * onehot, axis=1)
    destination = flat_experts * capacity + slot_index
    token_of = jnp.arange(moe_rows * TOP, dtype=jnp.int32) // TOP
    outgoing = (
        jnp.zeros((n_experts * capacity, normed.shape[1]), jnp.bfloat16)
        .at[destination]
        .set(normed[token_of])
    )
    outgoing = outgoing.reshape(n_experts, capacity, normed.shape[1])
    arrived = lax.all_to_all(outgoing, "seq", split_axis=0, concat_axis=0, tiled=True)
    sources = arrived.shape[0]
    slots = arrived.shape[1]
    inputs = arrived.reshape(sources * slots, arrived.shape[2])
    group = lax.all_gather(inputs, "exp", axis=0, tiled=True)
    gate_part = jnp.dot(group, w_gate[0], preferred_element_type=jnp.float32)
    up_part = jnp.dot(group, w_up[0], preferred_element_type=jnp.float32)
    act = (jax.nn.silu(gate_part) * up_part).astype(jnp.bfloat16)
    result = lax.psum_scatter(
        jnp.dot(act, w_down[0], preferred_element_type=jnp.float32).astype(jnp.bfloat16),
        "exp",
        scatter_dimension=0,
        tiled=True,
    )
    result = result.reshape(sources, slots, result.shape[1])
    back = send_back(result)
    gathered = back.reshape(n_experts * capacity, back.shape[2])[destination]
    gathered = gathered.reshape(moe_rows, TOP, gathered.shape[1]).astype(jnp.float32)
    mixture = jnp.einsum("mk,mkd->md", gates, gathered)
    return (stream + mixture).astype(jnp.bfloat16)


def solution(mesh):
    in_specs = (
        P("seq", "exp"),
        P("seq", "exp"),
        P("seq", "exp"),
        P(("seq", "exp"), None),
        P(),
        P("exp", None),
        P(),
        P(("seq", "exp"), None),
        P(("seq", "exp"), None),
        P("seq", None, "exp"),
        P("seq", None, "exp"),
        P("seq", "exp", None),
    )
    out_specs = P(("seq", "exp"), None)
    return jax.shard_map(shards, mesh=mesh, in_specs=in_specs, out_specs=out_specs, check_vma=False)
```

profile of v0, /device:TPU:1, one launch (start us, length us, event | category | flops | bytes accessed | tf_op | source)
XLA Modules:
  0.0 380.7 jit_solution(15358219397726013312)
XLA Ops:
  6.5 0.0 copy-start
  6.5 0.0 all-reduce.3.cloned.1.call-start
  6.5 1.2 copy.16
  7.8 1.1 copy.17
  8.9 0.1 pad_maximum_fusion.1
  8.9 4.8 %collective-permute-start = (bf16[2,256,512]{1,2,0:T(8,128)(2,1)S(1)}, bf16[2,256,512]{1,2,0:T(8,128)(2,1)}, u32[]{:S(2)}, u32[]{:S(2)}) collective-permute-start(bf16[2,256,512]{1,2,0:T(8,128)(2,1)S(1)} %pad_maximum_fusion.1), channel_id=1, source_target_pairs={{0,2},{2,4},{4,6},{6,8},{8,10},{10,12},{12,14},{14,16},{16,18},{18... | collective-permute-start | bytes 1572872 | tf_op jit(solution)/shard_map/ppermute | solution.py:20
  13.7 1.3 collective-permute-start.1
  15.0 0.8 pad_dynamic-slice_fusion.1
  15.8 0.8 pad_dynamic-slice_fusion
  16.5 0.3 fusion.18
  16.8 0.0 copy-start.4
  16.8 6.6 %collective-permute-done = bf16[2,256,512]{1,2,0:T(8,128)(2,1)} collective-permute-done((bf16[2,256,512]{1,2,0:T(8,128)(2,1)S(1)}, bf16[2,256,512]{1,2,0:T(8,128)(2,1)}, u32[]{:S(2)}, u32[]{:S(2)}) %collective-permute-start) | collective-permute-done | bytes 524320 | tf_op jit(solution)/shard_map/ppermute | solution.py:20
  23.5 4.7 %collective-permute-done.1 = bf16[2,256,512]{1,2,0:T(8,128)(2,1)} collective-permute-done((bf16[2,256,512]{1,2,0:T(8,128)(2,1)S(1)}, bf16[2,256,512]{1,2,0:T(8,128)(2,1)}, u32[]{:S(2)}, u32[]{:S(2)}) %collective-permute-start.1) | collective-permute-done | bytes 524320 | tf_op jit(solution)/shard_map/ppermute | solution.py:22
  28.2 1.3 pad_maximum_fusion
  29.5 0.1 fusion.31
  29.6 0.0 copy-done.4
  29.6 0.6 fusion.19
  30.2 1.6 fusion.32
  31.8 0.4 fusion.16
  32.2 0.0 copy-start.5
  32.2 0.0 copy-start.2
  32.2 0.0 copy-done
  32.3 0.0 copy-start.6
  32.3 1.7 convolution_convert_fusion.1
  34.0 0.0 all-reduce.3.cloned.1.call-update
  34.0 0.0 all-gather.2.cloned.1.call-start
  34.1 0.0 copy-done.5
  34.1 0.1 copy.22
  34.2 0.1 eq.49
  34.3 0.1 eq.45
  34.5 1.8 reduce-window.6
  36.3 0.3 slice_reduce_fusion
  36.6 0.1 copy.21
  36.7 0.1 mul.56
  36.9 0.1 fusion.24
  37.1 28.8 %all-reduce.3.cloned.1.call-done = bf16[256,2048]{1,0:T(8,128)(2,1)} async-done(((bf16[256,2048]{1,0:T(8,128)(2,1)}), bf16[256,2048]{1,0:T(8,128)(2,1)}) %all-reduce.3.cloned.1.call-update) | async-done | bytes 1048592 | tf_op jit(solution)/shard_map/psum | solution.py:74
  65.9 0.0 copy-done.2
  65.9 1.3 multiply_reduce_fusion
  67.2 0.0 copy-done.6
  67.2 1.3 multiply_convert_fusion
  68.5 24.2 %scatter_custom_fusion = bf16[1536,2048]{1,0:T(8,128)(2,1)} fusion(s32[768]{0:T(1024)S(1)} %fusion.26, bf16[128,2048]{1,0:T(8,128)(2,1)S(1)} %multiply_convert_fusion, s32[1024]{0:T(1024)S(1)} %pad_clamp_fusion.1, bf16[]{:T(256)} %constant.50.clone.1), kind=kCustom, calls=%fused_computation.8 | custom fusion | bytes 6291458 | tf_op jit(solution)/shard_map/scatter | solution.py:95
  92.7 84.5 %all_to_all.10 = bf16[64,24,2048]{2,1,0:T(8,128)(2,1)} all-to-all(bf16[64,24,2048]{2,1,0:T(8,128)(2,1)} %bitcast.73), channel_id=1, replica_groups=mesh['seq'=64,'exp'=2] {'seq'}, dimensions={0} | all-to-all | bytes 12582912 | tf_op jit(solution)/shard_map/all_to_all | solution.py:98
  177.1 0.0 copy-start.8
  177.1 0.0 all-gather.2.cloned.1.call-update
  177.1 0.0 reduce-scatter.2.cloned.1.call-start
  177.2 25.9 %all-gather.2.cloned.1.call-done = bf16[3072,2048]{1,0:T(8,128)(2,1)} async-done(((bf16[1536,2048]{1,0:T(8,128)(2,1)}), bf16[3072,2048]{1,0:T(8,128)(2,1)}) %all-gather.2.cloned.1.call-update) | async-done | bytes 12582928 | tf_op jit(solution)/shard_map/all_gather | solution.py:102
  203.1 0.0 copy-done.8
  203.1 9.8 %fusion.14 = f32[3072,352]{0,1:T(8,128)} fusion(bf16[3072,2048]{1,0:T(8,128)(2,1)} %all-gather.2.cloned.1.call-done, bf16[1,2048,352]{1,2,0:T(8,128)(2,1)S(1)} %copy-done.8), kind=kOutput, calls=%fused_computation.23 | convolution fusion | flops 4429185024 | bytes 18350080 | tf_op jit(solution)/shard_map/dot_general | solution.py:103
  212.9 18.6 %convolution_convert_fusion = bf16[3072,2048]{1,0:T(8,128)(2,1)} fusion(bf16[3072,2048]{1,0:T(8,128)(2,1)} %all-gather.2.cloned.1.call-done, f32[3072,352]{0,1:T(8,128)} %fusion.14, bf16[1,352,2048]{2,1,0:T(8,128)(2,1)} %param.23, bf16[1,2048,352]{1,2,0:T(8,128)(2,1)} %param.22), kind=kOutput, calls=%fused_computation.4 | convolution fusion | flops 8871149568 | bytes 32374784 | tf_op jit(solution)/shard_map/dot_general | solution.py:107
  231.5 0.0 reduce-scatter.2.cloned.1.call-update
  231.5 25.6 %reduce-scatter.2.cloned.1.call-done = bf16[1536,2048]{1,0:T(8,128)(2,1)} async-done(((bf16[3072,2048]{1,0:T(8,128)(2,1)}), bf16[1536,2048]{1,0:T(8,128)(2,1)}) %reduce-scatter.2.cloned.1.call-update) | async-done | bytes 6291472 | tf_op jit(solution)/shard_map/reduce_scatter | solution.py:106
  257.1 0.0 copy-start.7
  257.1 10.8 %all-to-all-start.1 = ((bf16[64,24,2048]{2,1,0:T(8,128)(2,1)}), bf16[64,24,2048]{2,1,0:T(8,128)(2,1)}, u32[]{:S(2)}, u32[]{:S(2)}) async-start(bf16[64,24,2048]{2,1,0:T(8,128)(2,1)} %bitcast.74), calls=%async_computation.2 | async-start | bytes 12582912 | tf_op jit(solution)/shard_map/all_to_all | solution.py:30
  268.0 0.0 copy-done.7
  268.0 0.2 copy.27
  268.1 84.1 %all-to-all-done.1 = bf16[64,24,2048]{2,1,0:T(8,128)(2,1)} async-done(((bf16[64,24,2048]{2,1,0:T(8,128)(2,1)}), bf16[64,24,2048]{2,1,0:T(8,128)(2,1)}, u32[]{:S(2)}, u32[]{:S(2)}) %all-to-all-start.1) | async-done | bytes 6291488 | tf_op jit(solution)/shard_map/all_to_all | solution.py:30
  352.2 10.8 %gather_fusion = bf16[768,2048]{1,0:T(8,128)(2,1)} fusion(bf16[1536,2048]{1,0:T(8,128)(2,1)} %bitcast.14, s32[1024]{0:T(1024)S(1)} %pad_clamp_fusion), kind=kCustom, calls=%fused_computation.1 | custom fusion | bytes 6294528 | tf_op jit(solution)/shard_map/gather | solution.py:114
  363.0 0.0 copy-start.1
  363.0 6.4 %reshape.179 = bf16[128,6,2048]{2,1,0:T(8,128)(2,1)} reshape(bf16[768,2048]{1,0:T(8,128)(2,1)} %gather_fusion) | data formatting | bytes 6291456 | tf_op jit(solution)/shard_map/reshape | solution.py:115
  369.4 0.0 copy-start.3
  369.4 3.5 fusion.33
  372.9 0.0 copy-done.3
  372.9 1.3 fusion.17
  374.2 0.0 copy-done.1
  (8 shorter events, 0.1 us)
Async XLA Ops:
  6.5 25.7 %copy-start = (bf16[512,2048]{1,0:T(8,128)(2,1)S(1)}, bf16[512,2048]{1,0:T(8,128)(2,1)}, u32[]{:S(2)}) copy-start(bf16[512,2048]{1,0:T(8,128)(2,1)} %param.17) | copy-start | bytes 6291460
  6.5 59.3 %all-reduce.3.cloned.1.call-start = ((), (), s32[]{:S(2)}) async-start(), calls=%async_computation.3 | async-start | bytes 2097152 | tf_op jit(solution)/shard_map/psum | solution.py:74
  8.9 14.5 %collective-permute-start = (bf16[2,256,512]{1,2,0:T(8,128)(2,1)S(1)}, bf16[2,256,512]{1,2,0:T(8,128)(2,1)}, u32[]{:S(2)}, u32[]{:S(2)}) collective-permute-start(bf16[2,256,512]{1,2,0:T(8,128)(2,1)S(1)} %pad_maximum_fusion.1), channel_id=1, source_target_pairs={{0,2},{2,4},{4,6},{6,8},{8,10},{10,12},{12,14},{14,16},{16,18},{18... | collective-permute-start | bytes 1572872 | tf_op jit(solution)/shard_map/ppermute | solution.py:20
  13.7 14.5 %collective-permute-start.1 = (bf16[2,256,512]{1,2,0:T(8,128)(2,1)S(1)}, bf16[2,256,512]{1,2,0:T(8,128)(2,1)}, u32[]{:S(2)}, u32[]{:S(2)}) collective-permute-start(bf16[2,256,512]{1,2,0:T(8,128)(2,1)S(1)} %pad_maximum_fusion.1), channel_id=1, source_target_pairs={{2,0},{4,2},{6,4},{8,6},{10,8},{12,10},{14,12},{16,14},{18,16},{20... | collective-permute-start | bytes 1572872 | tf_op jit(solution)/shard_map/ppermute | solution.py:22
  16.8 12.8 %copy-start.4 = (bf16[256,512]{1,0:T(8,128)(2,1)S(1)}, bf16[256,512]{1,0:T(8,128)(2,1)}, u32[]{:S(2)}) copy-start(bf16[256,512]{1,0:T(8,128)(2,1)} %param.12) | copy-start | bytes 786436
  32.2 1.9 copy-start.5
  32.2 33.7 %copy-start.2 = (bf16[128,2048]{1,0:T(8,128)(2,1)S(1)}, bf16[128,2048]{1,0:T(8,128)(2,1)}, u32[]{:S(2)}) copy-start(bf16[128,2048]{1,0:T(8,128)(2,1)} %param.15) | copy-start | bytes 1572868
  32.3 34.9 %copy-start.6 = (f32[2048]{0:T(1024)S(1)}, f32[2048]{0:T(1024)}, u32[]{:S(2)}) copy-start(f32[2048]{0:T(1024)} %param.18) | copy-start | bytes 24580
  34.0 169.1 %all-gather.2.cloned.1.call-start = ((), (), s32[]{:S(2)}) async-start(), calls=%async_computation.4 | async-start | bytes 18874368 | tf_op jit(solution)/shard_map/all_gather | solution.py:102
  177.1 26.0 %copy-start.8 = (bf16[1,2048,352]{1,2,0:T(8,128)(2,1)S(1)}, bf16[1,2048,352]{1,2,0:T(8,128)(2,1)}, u32[]{:S(2)}) copy-start(bf16[1,2048,352]{1,2,0:T(8,128)(2,1)} %param.21) | copy-start | bytes 4325380
  177.1 80.0 %reduce-scatter.2.cloned.1.call-start = ((), (), s32[]{:S(2)}) async-start(), calls=%async_computation.5 | async-start | bytes 18874368 | tf_op jit(solution)/shard_map/reduce_scatter | solution.py:106
  257.1 10.9 %copy-start.7 = (f32[128,6]{0,1:T(8,128)S(1)}, f32[128,6]{0,1:T(8,128)}, u32[]{:S(2)}) copy-start(f32[128,6]{0,1:T(8,128)} %param.20) | copy-start | bytes 9220
  257.1 95.1 %all-to-all-start.1 = ((bf16[64,24,2048]{2,1,0:T(8,128)(2,1)}), bf16[64,24,2048]{2,1,0:T(8,128)(2,1)}, u32[]{:S(2)}, u32[]{:S(2)}) async-start(bf16[64,24,2048]{2,1,0:T(8,128)(2,1)} %bitcast.74), calls=%async_computation.2 | async-start | bytes 12582912 | tf_op jit(solution)/shard_map/all_to_all | solution.py:30
  363.0 11.2 %copy-start.1 = (bf16[512,2048]{1,0:T(8,128)(2,1)S(1)}, bf16[512,2048]{1,0:T(8,128)(2,1)}, u32[]{:S(2)}) copy-start(bf16[512,2048]{1,0:T(8,128)(2,1)} %param.17) | copy-start | bytes 6291460
  369.4 3.5 copy-start.3
Sparse Core Ops, SparseCore 0:
  34.1 31.6 all-reduce.2
  177.3 25.7 all-gather.1
  231.6 25.4 reduce-scatter.1
where the time goes:
time: 384 us; the launch traced here: 381 us
  waiting for transfers between devices  176 us (46%)
  blocking collectives  84.5 us (22%)
  local copies, waits for them, and re-layouts  45.7 us (12%)
  matrix products  34.6 us (9%)
  starting transfers between devices  17 us (4%)
  between operations  13.4 us (3%)
  other arithmetic  9.89 us (3%)
    all_to_all x1, blocking collectives, shards(): lax.all_to_all(outgoing, 'seq', split_axis=0, concat_axis=0, tiled=True)  84.5 us
    all_to_all x1, waiting for transfers between devices, send_back(): lax.all_to_all(result, 'seq', split_axis=0, concat_axis=0, tiled=True)  84.1 us
    psum x1, waiting for transfers between devices, shards(): lax.psum(jnp.dot(attended, out_weight, preferred_element_type=jnp.float32...  28.8 us
    all_gather x1, waiting for transfers between devices, shards(): group = lax.all_gather(inputs, 'exp', axis=0, tiled=True)  25.9 us
    reduce_scatter x1, waiting for transfers between devices, shards(): lax.psum_scatter(jnp.dot(act, w_down[0], preferred_element_type=jnp.float...  25.6 us
    scatter x1, local copies, waits for them, and re-layouts, shards(): outgoing = jnp.zeros((n_experts * capacity, normed.shape[1]), jnp.bfloat1...  24.2 us
    dot_general x1, matrix products, shards(): jnp.dot(act, w_down[0], preferred_element_type=jnp.float32)  18.6 us
    all_to_all x1, starting transfers between devices, send_back(): lax.all_to_all(result, 'seq', split_axis=0, concat_axis=0, tiled=True)  10.8 us
  transfers between devices with their start and end apart: 6, of which 6 were waited for; matrix products, arithmetic and copies ran while one was open for 1% of the time, Pallas kernels for 0%

commit v1 on v0

v1 whole, which is shorter than its diff:
```python
import math

import jax
import jax.numpy as jnp
from jax import lax
from jax.sharding import PartitionSpec as P

HD = 128
TOP = 6
SWAP = [(0, 1), (1, 0)]


def with_halo(cells, axis, dim, width):
    count = lax.axis_size(axis)
    ends = count - 1
    head = lax.slice_in_dim(cells, 0, width, axis=dim)
    tail = lax.slice_in_dim(cells, cells.shape[dim] - width, cells.shape[dim], axis=dim)
    return jnp.concatenate(
        [
            lax.ppermute(tail, axis, [(i, (i + 1) % count) for i in range(ends)]),
            cells,
            lax.ppermute(head, axis, [((i + 1) % count, i) for i in range(ends)]),
        ],
        axis=dim,
    )


def swap(block):
    return lax.ppermute(block, "exp", SWAP)


def attention(queries, keys, values, pair_ids):
    tok_rows, local_width = queries.shape
    local_heads = local_width // HD
    shard = lax.axis_index("seq")
    widened = with_halo(jnp.stack([keys, values]), "seq", 1, tok_rows)
    id_pad = jnp.pad(pair_ids, (tok_rows, tok_rows), constant_values=-1)
    key_ids = lax.dynamic_slice_in_dim(id_pad, shard * tok_rows, 3 * tok_rows, 0)
    query_ids = lax.dynamic_slice_in_dim(id_pad, shard * tok_rows + tok_rows, tok_rows, 0)
    query_pos = jnp.arange(tok_rows, dtype=jnp.int32) + tok_rows
    key_pos = jnp.arange(3 * tok_rows, dtype=jnp.int32)
    allowed = (query_ids[:, None] == key_ids[None, :]) & (
        jnp.abs(query_pos[:, None] - key_pos[None, :]) < tok_rows
    )
    query_heads = queries.reshape(tok_rows, local_heads, HD)
    key_heads = widened[0].reshape(3 * tok_rows, local_heads, HD)
    value_heads = widened[1].reshape(3 * tok_rows, local_heads, HD)
    score = jnp.einsum(
        "qhd,khd->hqk", query_heads, key_heads, preferred_element_type=jnp.float32
    ) / math.sqrt(HD)
    score = jnp.where(allowed[None], score, -jnp.inf)
    top = jnp.max(score, axis=-1, keepdims=True)
    weights = jnp.exp(score - top)
    probs = (weights / jnp.sum(weights, axis=-1, keepdims=True)).astype(jnp.bfloat16)
    attended = jnp.einsum("hqk,khd->qhd", probs, value_heads, preferred_element_type=jnp.float32)
    return attended.reshape(tok_rows, local_width).astype(jnp.bfloat16)


def routing(experts, gates, n_experts, capacity):
    rows = experts.shape[0]
    names = jnp.arange(n_experts, dtype=jnp.int32)
    hits = experts[:, :, None] == names[None, None, :]
    named = jnp.sum(hits.astype(jnp.float32), axis=1)
    weight = jnp.sum(jnp.where(hits, gates[:, :, None], 0.0), axis=1)
    order = jnp.arange(rows, dtype=jnp.int32)
    before = (order[None, :] < order[:, None]).astype(jnp.bfloat16)
    ranks = jnp.dot(before, named.astype(jnp.bfloat16), preferred_element_type=jnp.float32)
    ranks = jnp.where(named > 0.0, ranks, -1.0)
    slots = jnp.arange(capacity, dtype=jnp.int32).astype(jnp.float32)
    chosen = ranks.T[:, None, :] == slots[None, :, None]
    pick = jnp.where(chosen, 1.0, 0.0).reshape(n_experts * capacity, rows).astype(jnp.bfloat16)
    blend = jnp.where(chosen, weight.T[:, None, :], 0.0)
    blend = blend.reshape(n_experts * capacity, rows).astype(jnp.bfloat16)
    return pick, blend


def shards(
    queries,
    keys,
    values,
    resid,
    pair_ids,
    out_weight,
    norm_gain,
    experts,
    gates,
    w_gate,
    w_up,
    w_down,
):
    moe_rows = resid.shape[0]
    n_experts = lax.axis_size("seq") * w_gate.shape[0]
    capacity = 2 * moe_rows * TOP // n_experts
    core = lax.axis_index("exp")
    attended = attention(queries, keys, values, pair_ids)
    mine = lax.dynamic_slice_in_dim(attended, core * moe_rows, moe_rows, 0)
    yours = swap(lax.dynamic_slice_in_dim(attended, (1 - core) * moe_rows, moe_rows, 0))
    out_other = swap(out_weight)
    gate_other, up_other, down_other = swap(w_gate[0]), swap(w_up[0]), swap(w_down[0])
    stream = (
        resid.astype(jnp.float32)
        + jnp.dot(mine, out_weight, preferred_element_type=jnp.float32)
        + jnp.dot(yours, out_other, preferred_element_type=jnp.float32)
    )
    meansq = jnp.mean(stream * stream, axis=-1, keepdims=True)
    normed = (stream * lax.rsqrt(meansq + 1e-05) * norm_gain).astype(jnp.bfloat16)
    pick, blend = routing(experts, gates, n_experts, capacity)
    outgoing = jnp.dot(pick, normed, preferred_element_type=jnp.float32).astype(jnp.bfloat16)
    outgoing = outgoing.reshape(n_experts, capacity, normed.shape[1])
    arrived = lax.all_to_all(outgoing, "seq", split_axis=0, concat_axis=0, tiled=True)
    inputs = arrived.reshape(n_experts * capacity, arrived.shape[2])

    def half(w_g, w_u, w_d):
        gate_part = jnp.dot(inputs, w_g, preferred_element_type=jnp.float32)
        up_part = jnp.dot(inputs, w_u, preferred_element_type=jnp.float32)
        act = (jax.nn.silu(gate_part) * up_part).astype(jnp.bfloat16)
        return jnp.dot(act, w_d, preferred_element_type=jnp.float32)

    result = half(w_gate[0], w_up[0], w_down[0]) + half(gate_other, up_other, down_other)
    result = result.astype(jnp.bfloat16).reshape(n_experts, capacity, arrived.shape[2])
    back = lax.all_to_all(result, "seq", split_axis=0, concat_axis=0, tiled=True)
    back = back.reshape(n_experts * capacity, back.shape[2])
    mixture = lax.dot_general(
        blend, back, (((0,), (0,)), ((), ())), preferred_element_type=jnp.float32
    )
    return (stream + mixture).astype(jnp.bfloat16)


def solution(mesh):
    in_specs = (
        P("seq", "exp"),
        P("seq", "exp"),
        P("seq", "exp"),
        P(("seq", "exp"), None),
        P(),
        P("exp", None),
        P(),
        P(("seq", "exp"), None),
        P(("seq", "exp"), None),
        P("seq", None, "exp"),
        P("seq", None, "exp"),
        P("seq", "exp", None),
    )
    out_specs = P(("seq", "exp"), None)
    return jax.shard_map(shards, mesh=mesh, in_specs=in_specs, out_specs=out_specs, check_vma=False)
```

time: 384 us -> 259 us (0.67)
  waiting for transfers between devices: 176 us -> 82.4 us
  local copies, waits for them, and re-layouts: 45.7 us -> 3.64 us
  matrix products: 34.6 us -> 49.4 us
  between operations: 13.4 us -> 0.18 us
  starting transfers between devices: 17 us -> 28.3 us
  other arithmetic: 9.89 us -> 5.05 us
  blocking collectives: 84.5 us -> 88.7 us
    psum x1 -> x0, waiting for transfers between devices: 28.8 us -> none  [shards(): lax.psum(jnp.dot(attended, out_weight, preferred_element_type=jnp.float32...]
    all_gather x1 -> x0, waiting for transfers between devices: 25.9 us -> none  [shards(): group = lax.all_gather(inputs, 'exp', axis=0, tiled=True)]
    reduce_scatter x1 -> x0, waiting for transfers between devices: 25.6 us -> none  [shards(): lax.psum_scatter(jnp.dot(act, w_down[0], preferred_element_type=jnp.float...]
    scatter x1 -> x0, local copies, waits for them, and re-layouts: 24.2 us -> none  [shards(): outgoing = jnp.zeros((n_experts * capacity, normed.shape[1]), jnp.bfloat1...]
    dot_general x6 -> x11, matrix products: 34.6 us -> 49.4 us  [the longest x2 27.1 us: half(): return jnp.dot(act, w_d, preferred_element_type=jnp.float32)]
    gather x1 -> x0, local copies, waits for them, and re-layouts: 10.8 us -> none  [shards(): gathered = back.reshape(n_experts * capacity, back.shape[2])[destination]]
    all_to_all x1, waiting for transfers between devices: 84.1 us -> 77.5 us  [shards(): lax.all_to_all(outgoing, 'seq', split_axis=0, concat_axis=0, tiled=True)]
    reshape x1 -> x0, local copies, waits for them, and re-layouts: 6.4 us -> none  [shards(): gathered.reshape(moe_rows, TOP, gathered.shape[1]).astype(jnp.float32)]
  transfers between devices with their start and end apart: 6 -> 8, of which waited for: 6 -> 4; matrix products, arithmetic and copies ran while one was open for 1% -> 13% of each run, Pallas kernels for 0% -> 0%
where the time goes in v1:
time: 259 us; the launch traced here: 258 us
  blocking collectives  88.7 us (34%)
  waiting for transfers between devices  82.4 us (32%)
  matrix products  49.4 us (19%)
  starting transfers between devices  28.3 us (11%)
  other arithmetic  5.05 us (2%)
  local copies, waits for them, and re-layouts  3.64 us (1%)
    all_to_all x1, blocking collectives, shards(): lax.all_to_all(result, 'seq', split_axis=0, concat_axis=0, tiled=True)  88.7 us
    all_to_all x1, waiting for transfers between devices, shards(): lax.all_to_all(outgoing, 'seq', split_axis=0, concat_axis=0, tiled=True)  77.5 us
    dot_general x2, matrix products, half(): return jnp.dot(act, w_d, preferred_element_type=jnp.float32)  27.1 us
    all_to_all x1, starting transfers between devices, shards(): lax.all_to_all(outgoing, 'seq', split_axis=0, concat_axis=0, tiled=True)  16.5 us
    dot_general x2, matrix products, half(): gate_part = jnp.dot(inputs, w_g, preferred_element_type=jnp.float32)  13.6 us
    ppermute x1, starting transfers between devices, with_halo(): lax.ppermute(tail, axis, [(i, (i + 1) % count) for i in range(ends)])  5.36 us
  transfers between devices with their start and end apart: 8, of which 4 were waited for; matrix products, arithmetic and copies ran while one was open for 13% of the time, Pallas kernels for 0%

profile of v1, /device:TPU:1, one launch (start us, length us, event | category | flops | bytes accessed | tf_op | source)
XLA Modules:
  0.0 257.6 jit_solution(11701290112565859225)
XLA Ops:
  0.0 0.0 copy-start
  0.0 0.0 copy-start.4
  0.0 1.1 copy.35
  1.1 1.1 copy.36
  2.2 0.1 pad_maximum_fusion.1
  2.3 1.3 collective-permute-start.1
  3.6 5.4 %collective-permute-start = (bf16[2,256,512]{1,2,0:T(8,128)(2,1)S(1)}, bf16[2,256,512]{1,2,0:T(8,128)(2,1)}, u32[]{:S(2)}, u32[]{:S(2)}) collective-permute-start(bf16[2,256,512]{1,2,0:T(8,128)(2,1)S(1)} %pad_maximum_fusion.1), channel_id=1, source_target_pairs={{0,2},{2,4},{4,6},{6,8},{8,10},{10,12},{12,14},{14,16},{16,18},{18... | collective-permute-start | bytes 1572872 | tf_op jit(solution)/shard_map/ppermute | solution.py:20
  9.0 1.4 collective-permute-start.3
  10.3 0.7 select_reduce_fusion
  11.1 0.1 convolution_select_fusion
  11.2 0.0 copy-start.6
  11.2 0.5 copy-done.6
  11.7 0.7 eq.67
  12.4 1.0 select_convert_fusion
  13.4 0.0 copy-done.4
  13.4 0.1 pad_dynamic-slice_fusion.1
  13.5 0.1 pad_dynamic-slice_fusion
  13.6 0.3 fusion.13
  13.9 3.6 %collective-permute-done.1 = bf16[2,256,512]{1,2,0:T(8,128)(2,1)} collective-permute-done((bf16[2,256,512]{1,2,0:T(8,128)(2,1)S(1)}, bf16[2,256,512]{1,2,0:T(8,128)(2,1)}, u32[]{:S(2)}, u32[]{:S(2)}) %collective-permute-start.1) | collective-permute-done | bytes 524320 | tf_op jit(solution)/shard_map/ppermute | solution.py:22
  17.5 0.8 collective-permute-done
  18.3 1.3 pad_maximum_fusion
  19.6 0.1 fusion.36
  19.7 0.0 copy-done
  19.7 0.6 fusion.20
  20.3 1.6 fusion.37
  21.9 0.0 copy-start.2
  21.9 0.0 copy-start.3
  21.9 0.4 fusion.10
  22.4 2.1 collective-permute-start.2
  24.5 0.0 copy-done.2
  24.5 0.0 copy-done.3
  24.5 0.5 convolution_add_fusion.1
  25.0 0.0 copy-start.5
  25.0 0.5 collective-permute-done.2
  25.5 0.0 collective-permute-done.3
  25.5 0.5 multiply_reduce_fusion
  26.1 0.0 copy-done.5
  26.1 4.5 %convolution_convert_fusion = bf16[1536,2048]{1,0:T(8,128)(2,1)} fusion(bf16[1536,128]{1,0:T(8,128)(2,1)S(1)} %select_convert_fusion, f32[128,2048]{1,0:T(8,128)S(1)} %get-tuple-element.12, f32[2048]{0:T(1024)S(1)} %copy-done.5, f32[128]{0:T(128)S(1)} %add_rsqrt_fusion), kind=kOutput, calls=%fused_computation.2 | convolution fusion | flops 809238528 | bytes 7741952 | tf_op jit(solution)/shard_map/dot_general | solution.py:108
  30.6 0.0 copy-start.8
  30.6 16.5 %all-to-all-start = ((bf16[64,24,2048]{2,1,0:T(8,128)(2,1)}), bf16[64,24,2048]{2,1,0:T(8,128)(2,1)}, u32[]{:S(2)}, u32[]{:S(2)}) async-start(bf16[64,24,2048]{2,1,0:T(8,128)(2,1)} %bitcast.65), calls=%async_computation | async-start | bytes 12582912 | tf_op jit(solution)/shard_map/all_to_all | solution.py:110
  47.1 0.0 copy-done.8
  47.1 1.1 collective-permute-start.4
  48.2 0.1 collective-permute-start.6
  48.3 0.4 collective-permute-start.5
  48.7 77.5 %all-to-all-done = bf16[64,24,2048]{2,1,0:T(8,128)(2,1)} async-done(((bf16[64,24,2048]{2,1,0:T(8,128)(2,1)}), bf16[64,24,2048]{2,1,0:T(8,128)(2,1)}, u32[]{:S(2)}, u32[]{:S(2)}) %all-to-all-start) | async-done | bytes 6291488 | tf_op jit(solution)/shard_map/all_to_all | solution.py:110
  126.2 6.5 %fusion.30 = f32[1536,352]{0,1:T(8,128)} fusion(bf16[1536,2048]{1,0:T(8,128)(2,1)} %bitcast.12, bf16[1,2048,352]{1,2,0:T(8,128)(2,1)S(1)} %copy-done.8), kind=kOutput, calls=%fused_computation.58 | convolution fusion | flops 2214592512 | bytes 9895936 | tf_op jit(solution)/shard_map/dot_general | solution.py:114
  132.8 0.0 collective-permute-done.4
  132.8 0.0 copy-start.9
  132.8 7.1 %fusion.40 = f32[1536,352]{0,1:T(8,128)} fusion(bf16[1536,2048]{1,0:T(8,128)(2,1)} %bitcast.12, bf16[2048,352]{0,1:T(8,128)(2,1)} %collective-permute-done.4), kind=kOutput, calls=%fused_computation.67 | convolution fusion | flops 2214592512 | bytes 9895936 | tf_op jit(solution)/shard_map/dot_general | solution.py:114
  139.9 0.0 copy-done.9
  139.9 12.8 %fusion.9 = f32[1536,2048]{1,0:T(8,128)} fusion(bf16[1536,2048]{1,0:T(8,128)(2,1)} %bitcast.12, f32[1536,352]{0,1:T(8,128)} %fusion.30, bf16[1,352,2048]{2,1,0:T(8,128)(2,1)S(1)} %copy-done.9, bf16[1,2048,352]{1,2,0:T(8,128)(2,1)} %param.22), kind=kOutput, calls=%fused_computation.20 | convolution fusion | flops 4432429056 | bytes 23920640 | tf_op jit(solution)/shard_map/dot_general | solution.py:117
  152.7 0.0 collective-permute-done.6
  152.7 0.0 collective-permute-done.5
  152.7 14.4 %add_convert_fusion = bf16[1536,2048]{1,0:T(8,128)(2,1)} fusion(f32[1536,2048]{1,0:T(8,128)} %fusion.9, bf16[352,2048]{1,0:T(8,128)(2,1)} %collective-permute-done.6, f32[1536,352]{0,1:T(8,128)} %fusion.40, bf16[1536,2048]{1,0:T(8,128)(2,1)} %bitcast.12, bf16[2048,352]{0,1:T(8,128)(2,1)} %collective-permute-done.5), kind=kOutput, calls=%fused_computation.1 | convolution fusion | flops 4438720512 | bytes 30212096 | tf_op jit(solution)/shard_map/dot_general | solution.py:117
  167.0 0.0 copy-start.7
  167.0 88.7 %all_to_all.10 = bf16[64,24,2048]{2,1,0:T(8,128)(2,1)S(1)} all-to-all(bf16[64,24,2048]{2,1,0:T(8,128)(2,1)} %bitcast.66), channel_id=1, replica_groups=mesh['seq'=64,'exp'=2] {'seq'}, dimensions={0} | all-to-all | bytes 12582912 | tf_op jit(solution)/shard_map/all_to_all | solution.py:121
  255.7 0.0 copy-start.1
  255.7 0.0 copy-done.7
  255.7 1.9 fusion.3
  257.6 0.0 copy-done.1
  (4 shorter events, 0.0 us)
Async XLA Ops:
  0.0 19.7 %copy-start = (bf16[256,512]{1,0:T(8,128)(2,1)S(1)}, bf16[256,512]{1,0:T(8,128)(2,1)}, u32[]{:S(2)}) copy-start(bf16[256,512]{1,0:T(8,128)(2,1)} %param.12) | copy-start | bytes 786436
  0.0 13.4 %copy-start.4 = (s32[16384]{0:T(1024)S(1)}, s32[16384]{0:T(1024)}, u32[]{:S(2)}) copy-start(s32[16384]{0:T(1024)} %param.16) | copy-start | bytes 196612
  2.3 15.2 %collective-permute-start.1 = (bf16[2,256,512]{1,2,0:T(8,128)(2,1)S(1)}, bf16[2,256,512]{1,2,0:T(8,128)(2,1)}, u32[]{:S(2)}, u32[]{:S(2)}) collective-permute-start(bf16[2,256,512]{1,2,0:T(8,128)(2,1)S(1)} %pad_maximum_fusion.1), channel_id=1, source_target_pairs={{2,0},{4,2},{6,4},{8,6},{10,8},{12,10},{14,12},{16,14},{18,16},{20... | collective-permute-start | bytes 1572872 | tf_op jit(solution)/shard_map/ppermute | solution.py:22
  3.6 14.7 %collective-permute-start = (bf16[2,256,512]{1,2,0:T(8,128)(2,1)S(1)}, bf16[2,256,512]{1,2,0:T(8,128)(2,1)}, u32[]{:S(2)}, u32[]{:S(2)}) collective-permute-start(bf16[2,256,512]{1,2,0:T(8,128)(2,1)S(1)} %pad_maximum_fusion.1), channel_id=1, source_target_pairs={{0,2},{2,4},{4,6},{6,8},{8,10},{10,12},{12,14},{14,16},{16,18},{18... | collective-permute-start | bytes 1572872 | tf_op jit(solution)/shard_map/ppermute | solution.py:20
  9.0 16.6 %collective-permute-start.3 = (bf16[512,2048]{1,0:T(8,128)(2,1)}, bf16[512,2048]{1,0:T(8,128)(2,1)S(1)}, u32[]{:S(2)}, u32[]{:S(2)}) collective-permute-start(bf16[512,2048]{1,0:T(8,128)(2,1)} %param.17), channel_id=1, source_target_pairs={{0,1},{1,0},{2,3},{3,2},{4,5},{5,4},{6,7},{7,6},{8,9},{9,8},{10,11... | collective-permute-start | bytes 6291464 | tf_op jit(solution)/shard_map/ppermute | solution.py:29
  11.2 0.5 copy-start.6
  21.9 2.6 %copy-start.2 = (bf16[512,2048]{1,0:T(8,128)(2,1)S(1)}, bf16[512,2048]{1,0:T(8,128)(2,1)}, u32[]{:S(2)}) copy-start(bf16[512,2048]{1,0:T(8,128)(2,1)} %param.17) | copy-start | bytes 6291460
  21.9 2.6 %copy-start.3 = (bf16[128,2048]{1,0:T(8,128)(2,1)S(1)}, bf16[128,2048]{1,0:T(8,128)(2,1)}, u32[]{:S(2)}) copy-start(bf16[128,2048]{1,0:T(8,128)(2,1)} %param.15) | copy-start | bytes 1572868
  22.4 3.1 %collective-permute-start.2 = (bf16[128,512]{0,1:T(8,128)(2,1)S(1)}, bf16[128,512]{0,1:T(8,128)(2,1)S(1)}, u32[]{:S(2)}, u32[]{:S(2)}) collective-permute-start(bf16[128,512]{0,1:T(8,128)(2,1)S(1)} %constant_dynamic-slice_fusion), channel_id=1, source_target_pairs={{0,1},{1,0},{2,3},{3,2},{4,5},{5,4},{6,7},{7,6},{8,9},{9,8},{10,11... | collective-permute-start | bytes 393224 | tf_op jit(solution)/shard_map/ppermute | solution.py:29
  25.0 1.1 copy-start.5
  30.6 16.5 %copy-start.8 = (bf16[1,2048,352]{1,2,0:T(8,128)(2,1)S(1)}, bf16[1,2048,352]{1,2,0:T(8,128)(2,1)}, u32[]{:S(2)}) copy-start(bf16[1,2048,352]{1,2,0:T(8,128)(2,1)} %param.21) | copy-start | bytes 4325380
  30.6 95.6 %all-to-all-start = ((bf16[64,24,2048]{2,1,0:T(8,128)(2,1)}), bf16[64,24,2048]{2,1,0:T(8,128)(2,1)}, u32[]{:S(2)}, u32[]{:S(2)}) async-start(bf16[64,24,2048]{2,1,0:T(8,128)(2,1)} %bitcast.65), calls=%async_computation | async-start | bytes 12582912 | tf_op jit(solution)/shard_map/all_to_all | solution.py:110
  47.1 85.6 %collective-permute-start.4 = (bf16[2048,352]{0,1:T(8,128)(2,1)S(1)}, bf16[2048,352]{0,1:T(8,128)(2,1)}, u32[]{:S(2)}, u32[]{:S(2)}) collective-permute-start(bf16[2048,352]{0,1:T(8,128)(2,1)S(1)} %bitcast.76), channel_id=1, source_target_pairs={{0,1},{1,0},{2,3},{3,2},{4,5},{5,4},{6,7},{7,6},{8,9},{9,8},{10,11... | collective-permute-start | bytes 4325384 | tf_op jit(solution)/shard_map/ppermute | solution.py:29
  48.2 104.5 %collective-permute-start.6 = (bf16[352,2048]{1,0:T(8,128)(2,1)}, bf16[352,2048]{1,0:T(8,128)(2,1)}, u32[]{:S(2)}, u32[]{:S(2)}) collective-permute-start(bf16[352,2048]{1,0:T(8,128)(2,1)} %bitcast.77), channel_id=1, source_target_pairs={{0,1},{1,0},{2,3},{3,2},{4,5},{5,4},{6,7},{7,6},{8,9},{9,8},{10,11... | collective-permute-start | bytes 4325384 | tf_op jit(solution)/shard_map/ppermute | solution.py:29
  48.3 104.4 %collective-permute-start.5 = (bf16[2048,352]{0,1:T(8,128)(2,1)}, bf16[2048,352]{0,1:T(8,128)(2,1)}, u32[]{:S(2)}, u32[]{:S(2)}) collective-permute-start(bf16[2048,352]{0,1:T(8,128)(2,1)} %bitcast.78), channel_id=1, source_target_pairs={{0,1},{1,0},{2,3},{3,2},{4,5},{5,4},{6,7},{7,6},{8,9},{9,8},{10,11... | collective-permute-start | bytes 4325384 | tf_op jit(solution)/shard_map/ppermute | solution.py:29
  132.8 7.1 %copy-start.9 = (bf16[1,352,2048]{2,1,0:T(8,128)(2,1)S(1)}, bf16[1,352,2048]{2,1,0:T(8,128)(2,1)}, u32[]{:S(2)}) copy-start(bf16[1,352,2048]{2,1,0:T(8,128)(2,1)} %param.23) | copy-start | bytes 4325380
  167.0 88.7 %copy-start.7 = (f32[24]{0:T(128)S(1)}, f32[24]{0:T(128)}, u32[]{:S(2)}) copy-start(f32[24]{0:T(128)} %copy-done.6) | copy-start | bytes 292
  255.7 1.9 copy-start.1

commit v2 on v1

--- a/solution.py
+++ b/solution.py
@@ -3,11 +3,16 @@
 import jax
 import jax.numpy as jnp
 from jax import lax
+from jax.experimental import pallas as pl
+from jax.experimental.pallas import tpu as pltpu
 from jax.sharding import PartitionSpec as P
 
 HD = 128
 TOP = 6
 SWAP = [(0, 1), (1, 0)]
+SIDE = 4
+AXES = ("z", "y", "x")
+ORDERS = ((2, 1, 0), (1, 0, 2), (0, 2, 1))
 
 
 def with_halo(cells, axis, dim, width):
@@ -29,6 +34,141 @@
     return lax.ppermute(block, "exp", SWAP)
 
 
+def peer(axis, delta):
+    me = lax.axis_index("seq")
+    at = [me // (SIDE * SIDE), (me // SIDE) % SIDE, me % SIDE]
+    at[axis] = (at[axis] + delta) % SIDE
+    return ((at[0] * SIDE + at[1]) * SIDE + at[2], lax.axis_index("exp"))
+
+
+def cell(group, **fixed):
+    return tuple(fixed.get(AXES[i], slice(None)) for i in range(3)) + (group,)
+
+
+def exchange_kernel(src, out, first, second, local_sem, send_sem, recv_sem):
+    barrier = pltpu.get_barrier_semaphore()
+    for axis in range(3):
+        for delta in range(1, SIDE):
+            pl.semaphore_signal(
+                barrier, inc=1, device_id=peer(axis, delta), device_id_type=pl.DeviceIdType.MESH
+            )
+    pl.semaphore_wait(barrier, 3 * (SIDE - 1))
+
+    used = [0]
+    sent = []
+
+    def send(axis, delta, source, target):
+        number = used[0]
+        used[0] += 1
+        copy = pltpu.make_async_remote_copy(
+            src_ref=source,
+            dst_ref=target,
+            send_sem=send_sem.at[number],
+            recv_sem=recv_sem.at[number],
+            device_id=peer(axis, delta),
+            device_id_type=pl.DeviceIdType.MESH,
+        )
+        copy.start()
+        sent.append(copy)
+        return copy
+
+    routes = [(g, ORDERS[g]) for g in range(3)]
+    deltas = (2, 1, 3)
+    one, two, three = {}, {}, []
+    for d in deltas:
+        for g, (a, b, c) in routes:
+            na = AXES[a]
+            one[g, d] = send(
+                a, d, src.at[cell(g, **{na: d})], first.at[cell(g, **{na: SIDE - d})]
+            )
+
+    def relay(i, g, d):
+        a, b, c = ORDERS[g]
+        na, nb = AXES[a], AXES[b]
+        held = src if i == 0 else first
+        two[g, i, d] = send(
+            b,
+            d,
+            held.at[cell(g, **{na: i, nb: d})],
+            second.at[cell(g, **{na: i, nb: SIDE - d})],
+        )
+
+    for d in deltas:
+        for g, _ in routes:
+            relay(0, g, d)
+    for i in (1, 3, 2):
+        for g, _ in routes:
+            one[g, SIDE - i].wait_recv()
+        for d in deltas:
+            for g, _ in routes:
+                relay(i, g, d)
+
+    def deliver(g, d, held, **at):
+        c = ORDERS[g][2]
+        nc = AXES[c]
+        three.append(
+            send(
+                c,
+                d,
+                held.at[cell(g, **{nc: d}, **at)],
+                out.at[cell(g, **{nc: SIDE - d}, **at)],
+            )
+        )
+
+    locals_ = []
+
+    def keep(g, held, **at):
+        nc = AXES[ORDERS[g][2]]
+        where = cell(g, **{nc: 0}, **at)
+        copy = pltpu.make_async_copy(held.at[where], out.at[where], local_sem.at[len(locals_)])
+        copy.start()
+        locals_.append(copy)
+
+    for i in range(SIDE):
+        for d in deltas:
+            for g, (a, b, c) in routes:
+                deliver(g, d, src if i == 0 else first, **{AXES[a]: i, AXES[b]: 0})
+    for j in (1, 3, 2):
+        for i in range(SIDE):
+            for g, _ in routes:
+                two[g, i, SIDE - j].wait_recv()
+        for d in deltas:
+            for g, (a, b, c) in routes:
+                deliver(g, d, second, **{AXES[b]: j})
+    for g, (a, b, c) in routes:
+        for i in range(SIDE):
+            keep(g, src if i == 0 else first, **{AXES[a]: i, AXES[b]: 0})
+        for j in range(1, SIDE):
+            keep(g, second, **{AXES[b]: j})
+    for copy in three:
+        copy.wait_recv()
+    for copy in locals_:
+        copy.wait()
+    for copy in sent:
+        copy.wait_send()
+
+
+def exchange(blocks, number):
+    copies = 3 * (3 + 4 * 3 + 3 * (4 + 3))
+    return pl.pallas_call(
+        exchange_kernel,
+        out_shape=jax.ShapeDtypeStruct(blocks.shape, blocks.dtype),
+        in_specs=[pl.BlockSpec(memory_space=pl.ANY)],
+        out_specs=pl.BlockSpec(memory_space=pl.ANY),
+        scratch_shapes=[
+            pltpu.VMEM(blocks.shape, blocks.dtype),
+            pltpu.VMEM(blocks.shape, blocks.dtype),
+            pltpu.SemaphoreType.DMA((3 * (4 + 3),)),
+            pltpu.SemaphoreType.DMA((copies,)),
+            pltpu.SemaphoreType.DMA((copies,)),
+        ],
+        compiler_params=pltpu.CompilerParams(
+            collective_id=number, has_side_effects=True, vmem_limit_bytes=20 << 20
+        ),
+        name="exchange_%d" % number,
+    )(blocks)
+
+
 def attention(queries, keys, values, pair_ids):
     tok_rows, local_width = queries.shape
     local_heads = local_width // HD
@@ -58,7 +198,13 @@
 
 def routing(experts, gates, n_experts, capacity):
     rows = experts.shape[0]
-    names = jnp.arange(n_experts, dtype=jnp.int32)
+    step = jnp.arange(n_experts, dtype=jnp.int32)
+    me = lax.axis_index("seq")
+    names = (
+        (step // 16 + me // 16) % SIDE * 16
+        + (step // 4 % SIDE + me // 4 % SIDE) % SIDE * 4
+        + (step % SIDE + me % SIDE) % SIDE
+    )
     hits = experts[:, :, None] == names[None, None, :]
     named = jnp.sum(hits.astype(jnp.float32), axis=1)
     weight = jnp.sum(jnp.where(hits, gates[:, :, None], 0.0), axis=1)
@@ -106,20 +252,18 @@
     normed = (stream * lax.rsqrt(meansq + 1e-05) * norm_gain).astype(jnp.bfloat16)
     pick, blend = routing(experts, gates, n_experts, capacity)
     outgoing = jnp.dot(pick, normed, preferred_element_type=jnp.float32).astype(jnp.bfloat16)
-    outgoing = outgoing.reshape(n_experts, capacity, normed.shape[1])
-    arrived = lax.all_to_all(outgoing, "seq", split_axis=0, concat_axis=0, tiled=True)
-    inputs = arrived.reshape(n_experts * capacity, arrived.shape[2])
-
-    def half(w_g, w_u, w_d):
-        gate_part = jnp.dot(inputs, w_g, preferred_element_type=jnp.float32)
-        up_part = jnp.dot(inputs, w_u, preferred_element_type=jnp.float32)
-        act = (jax.nn.silu(gate_part) * up_part).astype(jnp.bfloat16)
-        return jnp.dot(act, w_d, preferred_element_type=jnp.float32)
-
-    result = half(w_gate[0], w_up[0], w_down[0]) + half(gate_other, up_other, down_other)
-    result = result.astype(jnp.bfloat16).reshape(n_experts, capacity, arrived.shape[2])
-    back = lax.all_to_all(result, "seq", split_axis=0, concat_axis=0, tiled=True)
-    back = back.reshape(n_experts * capacity, back.shape[2])
+    width = normed.shape[1]
+    cells = (SIDE, SIDE, SIDE, 3, capacity // 3, width)
+    arrived = exchange(outgoing.reshape(cells), 0)
+    inputs = arrived.reshape(n_experts * capacity, width)
+    w_g = jnp.concatenate([w_gate[0], gate_other], axis=1)
+    w_u = jnp.concatenate([w_up[0], up_other], axis=1)
+    w_d = jnp.concatenate([w_down[0], down_other], axis=0)
+    gate_part = jnp.dot(inputs, w_g, preferred_element_type=jnp.float32)
+    up_part = jnp.dot(inputs, w_u, preferred_element_type=jnp.float32)
+    act = (jax.nn.silu(gate_part) * up_part).astype(jnp.bfloat16)
+    result = jnp.dot(act, w_d, preferred_element_type=jnp.float32).astype(jnp.bfloat16)
+    back = exchange(result.reshape(cells), 1).reshape(n_experts * capacity, width)
     mixture = lax.dot_general(
         blend, back, (((0,), (0,)), ((), ())), preferred_element_type=jnp.float32
     )

time: 259 us -> 218 us (0.84)
  Pallas kernels: 0 us -> 155 us
  blocking collectives: 88.7 us -> 0 us
  waiting for transfers between devices: 82.4 us -> 7.1 us
  starting transfers between devices: 28.3 us -> 10.3 us
  matrix products: 49.4 us -> 35.2 us
    pallas_call x0 -> x2, Pallas kernels: none -> 155 us  [exchange(): pl.pallas_call(exchange_kernel, out_shape=jax.ShapeDtypeStruct(blocks.sha...]
    all_to_all x1 -> x0, blocking collectives: 88.7 us -> none  [shards(): lax.all_to_all(result, 'seq', split_axis=0, concat_axis=0, tiled=True)]
    all_to_all x1 -> x0, waiting for transfers between devices: 77.5 us -> none  [shards(): lax.all_to_all(outgoing, 'seq', split_axis=0, concat_axis=0, tiled=True)]
    all_to_all x1 -> x0, starting transfers between devices: 16.5 us -> none  [shards(): lax.all_to_all(outgoing, 'seq', split_axis=0, concat_axis=0, tiled=True)]
    dot_general x4 -> x2, matrix products: 40.8 us -> 27.7 us  [the longest x1 18.9 us: shards(): jnp.dot(act, w_d, preferred_element_type=jnp.float32).astype(jnp.bfloat16)]
    ppermute x1, waiting for transfers between devices: 0.77 us -> 4.32 us  [with_halo(): lax.ppermute(tail, axis, [(i, (i + 1) % count) for i in range(ends)])]
    dot_general x1, matrix products: 4.54 us -> 1.87 us  [shards(): jnp.dot(pick, normed, preferred_element_type=jnp.float32)]
  transfers between devices with their start and end apart: 8 -> 7, of which waited for: 4 -> 3; matrix products, arithmetic and copies ran while one was open for 13% -> 9% of each run, Pallas kernels for 0% -> 36%
where the time goes in v2:
time: 218 us
  Pallas kernels  155 us (71%)
  matrix products  35.2 us (16%)
  starting transfers between devices  10.3 us (5%)
  waiting for transfers between devices  7.1 us (3%)
  local copies, waits for them, and re-layouts  6.04 us (3%)
  other arithmetic  4.1 us (2%)
    pallas_call x2, Pallas kernels, exchange(): pl.pallas_call(exchange_kernel, out_shape=jax.ShapeDtypeStruct(blocks.sha...  155 us
    dot_general x1, matrix products, shards(): jnp.dot(act, w_d, preferred_element_type=jnp.float32).astype(jnp.bfloat16)  18.9 us
    dot_general x1, matrix products, shards(): gate_part = jnp.dot(inputs, w_g, preferred_element_type=jnp.float32)  8.78 us
    unnamed x16, local copies, waits for them, and re-layouts  5.02 us
    ppermute x5, starting transfers between devices, swap(): return lax.ppermute(block, 'exp', SWAP)  5.02 us
  transfers between devices with their start and end apart: 7, of which 3 were waited for; matrix products, arithmetic and copies ran while one was open for 9% of the time, Pallas kernels for 36%

profile of v2, /device:TPU:1, one launch (start us, length us, event | category | flops | bytes accessed | tf_op | source)
XLA Modules:
  0.0 217.6 jit_solution(7534166117333668597)
XLA Ops:
  0.0 0.0 copy-start
  0.0 1.1 copy.25
  1.1 1.1 copy.26
  2.2 0.1 pad_maximum_fusion.1
  2.3 4.0 %collective-permute-start = (bf16[2,256,512]{1,2,0:T(8,128)(2,1)S(1)}, bf16[2,256,512]{1,2,0:T(8,128)(2,1)S(1)}, u32[]{:S(2)}, u32[]{:S(2)}) collective-permute-start(bf16[2,256,512]{1,2,0:T(8,128)(2,1)S(1)} %pad_maximum_fusion.1), channel_id=1, source_target_pairs={{0,2},{2,4},{4,6},{6,8},{8,10},{10,12},{12,14},{14,16},{16,18},{18... | collective-permute-start | bytes 1572872 | tf_op jit(solution)/shard_map/ppermute | solution.py:25
  6.3 1.3 collective-permute-start.1
  7.6 1.0 collective-permute-start.3
  8.6 0.1 collective-permute-start.4
  8.7 0.4 collective-permute-start.5
  9.1 0.8 fusion.32
  9.9 0.1 convolution_select_fusion
  10.1 0.1 eq.82
  10.2 0.8 pad_dynamic-slice_fusion
  11.0 0.3 select_convert_fusion
  11.3 0.8 pad_dynamic-slice_fusion.1
  12.0 0.3 fusion.26
  12.3 0.2 select_convert_fusion.1
  12.5 4.3 %collective-permute-done = bf16[2,256,512]{1,2,0:T(8,128)(2,1)S(1)} collective-permute-done((bf16[2,256,512]{1,2,0:T(8,128)(2,1)S(1)}, bf16[2,256,512]{1,2,0:T(8,128)(2,1)S(1)}, u32[]{:S(2)}, u32[]{:S(2)}) %collective-permute-start) | collective-permute-done | bytes 524320 | tf_op jit(solution)/shard_map/ppermute | solution.py:25
  16.8 1.5 collective-permute-start.6
  18.4 2.3 %collective-permute-done.1 = bf16[2,256,512]{1,2,0:T(8,128)(2,1)S(1)} collective-permute-done((bf16[2,256,512]{1,2,0:T(8,128)(2,1)S(1)}, bf16[2,256,512]{1,2,0:T(8,128)(2,1)S(1)}, u32[]{:S(2)}, u32[]{:S(2)}) %collective-permute-start.1) | collective-permute-done | bytes 524320 | tf_op jit(solution)/shard_map/ppermute | solution.py:27
  20.6 0.1 pad_maximum_fusion
  20.7 0.1 fusion.54
  20.9 0.0 copy-done
  20.9 0.6 fusion.29
  21.5 1.6 fusion.55
  23.1 0.0 copy-start.3
  23.1 0.0 copy-start.4
  23.1 0.4 fusion.25
  23.6 0.0 copy-start.5
  23.6 1.9 collective-permute-start.2
  25.5 0.0 copy-done.3
  25.5 0.0 copy-done.4
  25.5 0.5 convolution_add_fusion.1
  26.0 0.5 collective-permute-done.2
  26.5 0.0 collective-permute-done.3
  26.5 2.1 multiply_reduce_fusion
  28.7 0.0 copy-done.5
  28.7 1.9 convolution_convert_fusion.1
  30.6 0.0 copy-start.6
  30.6 79.1 %exchange_0.1 = bf16[4,4,4,3,8,2048]{5,4,3,2,1,0:T(8,128)(2,1)S(1)} custom-call(bf16[4,4,4,3,8,2048]{5,4,3,2,1,0:T(8,128)(2,1)S(1)} %bitcast.51), custom_call_target="tpu_custom_call" | custom-call | tf_op jit(solution)/shard_map/exchange_0/pallas_call | solution.py:153
  109.7 0.0 copy-start.1
  109.7 0.0 collective-permute-done.4
  109.7 0.0 copy-done.6
  109.8 8.8 %fusion.1 = f32[1536,704]{0,1:T(8,128)} fusion(bf16[1536,2048]{1,0:T(8,128)(2,1)S(1)} %bitcast.52, bf16[2048,352]{0,1:T(8,128)(2,1)} %collective-permute-done.4, bf16[2048,352]{0,1:T(8,128)(2,1)S(1)} %bitcast.66), kind=kOutput, calls=%fused_computation.7 | convolution fusion | flops 4434952192 | bytes 13500416 | tf_op jit(solution)/shard_map/dot_general | solution.py:262
  118.5 0.0 copy-done.1
  118.5 0.0 collective-permute-done.5
  118.5 0.0 collective-permute-done.6
  118.5 18.9 %convolution_convert_fusion = bf16[1536,2048]{1,0:T(8,128)(2,1)} fusion(f32[1536,704]{0,1:T(8,128)} %fusion.1, bf16[1536,2048]{1,0:T(8,128)(2,1)} %bitcast.53, bf16[2048,352]{0,1:T(8,128)(2,1)} %collective-permute-done.5, bf16[2048,352]{0,1:T(8,128)(2,1)} %bitcast.68, bf16[352,2048]{1,0:T(8,128)(2,1)} %collective-permute-done.6, bf16[352,2048]{1,0:T(8,128)(2,1)} %bitcast.70), kind=kOutput, calls=%fused_computation.1 | convolution fusion | flops 8879538176 | bytes 22675456 | tf_op jit(solution)/shard_map/dot_general | solution.py:265
  137.4 0.0 copy-start.2
  137.4 2.8 %copy-done.2 = bf16[1536,2048]{1,0:T(8,128)(2,1)S(1)} copy-done((bf16[1536,2048]{1,0:T(8,128)(2,1)S(1)}, bf16[1536,2048]{1,0:T(8,128)(2,1)}, u32[]{:S(2)}) %copy-start.2) | copy-done | bytes 6291480
  140.2 75.6 %exchange_1.1 = bf16[4,4,4,3,8,2048]{5,4,3,2,1,0:T(8,128)(2,1)S(1)} custom-call(bf16[4,4,4,3,8,2048]{5,4,3,2,1,0:T(8,128)(2,1)S(1)} %bitcast.54), custom_call_target="tpu_custom_call" | custom-call | tf_op jit(solution)/shard_map/exchange_1/pallas_call | solution.py:153
  215.8 1.8 fusion.18
  (5 shorter events, 0.0 us)
Async XLA Ops:
  0.0 20.9 %copy-start = (bf16[256,512]{1,0:T(8,128)(2,1)S(1)}, bf16[256,512]{1,0:T(8,128)(2,1)}, u32[]{:S(2)}) copy-start(bf16[256,512]{1,0:T(8,128)(2,1)} %param.12) | copy-start | bytes 786436
  2.3 14.5 %collective-permute-start = (bf16[2,256,512]{1,2,0:T(8,128)(2,1)S(1)}, bf16[2,256,512]{1,2,0:T(8,128)(2,1)S(1)}, u32[]{:S(2)}, u32[]{:S(2)}) collective-permute-start(bf16[2,256,512]{1,2,0:T(8,128)(2,1)S(1)} %pad_maximum_fusion.1), channel_id=1, source_target_pairs={{0,2},{2,4},{4,6},{6,8},{8,10},{10,12},{12,14},{14,16},{16,18},{18... | collective-permute-start | bytes 1572872 | tf_op jit(solution)/shard_map/ppermute | solution.py:25
  6.3 14.4 %collective-permute-start.1 = (bf16[2,256,512]{1,2,0:T(8,128)(2,1)S(1)}, bf16[2,256,512]{1,2,0:T(8,128)(2,1)S(1)}, u32[]{:S(2)}, u32[]{:S(2)}) collective-permute-start(bf16[2,256,512]{1,2,0:T(8,128)(2,1)S(1)} %pad_maximum_fusion.1), channel_id=1, source_target_pairs={{2,0},{4,2},{6,4},{8,6},{10,8},{12,10},{14,12},{16,14},{18,16},{20... | collective-permute-start | bytes 1572872 | tf_op jit(solution)/shard_map/ppermute | solution.py:27
  7.6 19.0 %collective-permute-start.3 = (bf16[512,2048]{1,0:T(8,128)(2,1)}, bf16[512,2048]{1,0:T(8,128)(2,1)}, u32[]{:S(2)}, u32[]{:S(2)}) collective-permute-start(bf16[512,2048]{1,0:T(8,128)(2,1)} %param.17), channel_id=1, source_target_pairs={{0,1},{1,0},{2,3},{3,2},{4,5},{5,4},{6,7},{7,6},{8,9},{9,8},{10,11... | collective-permute-start | bytes 6291464 | tf_op jit(solution)/shard_map/ppermute | solution.py:34
  8.6 101.1 %collective-permute-start.4 = (bf16[2048,352]{0,1:T(8,128)(2,1)}, bf16[2048,352]{0,1:T(8,128)(2,1)}, u32[]{:S(2)}, u32[]{:S(2)}) collective-permute-start(bf16[2048,352]{0,1:T(8,128)(2,1)} %bitcast.65), channel_id=1, source_target_pairs={{0,1},{1,0},{2,3},{3,2},{4,5},{5,4},{6,7},{7,6},{8,9},{9,8},{10,11... | collective-permute-start | bytes 4325384 | tf_op jit(solution)/shard_map/ppermute | solution.py:34
  8.7 109.8 %collective-permute-start.5 = (bf16[2048,352]{0,1:T(8,128)(2,1)}, bf16[2048,352]{0,1:T(8,128)(2,1)}, u32[]{:S(2)}, u32[]{:S(2)}) collective-permute-start(bf16[2048,352]{0,1:T(8,128)(2,1)} %bitcast.67), channel_id=1, source_target_pairs={{0,1},{1,0},{2,3},{3,2},{4,5},{5,4},{6,7},{7,6},{8,9},{9,8},{10,11... | collective-permute-start | bytes 4325384 | tf_op jit(solution)/shard_map/ppermute | solution.py:34
  16.8 101.7 %collective-permute-start.6 = (bf16[352,2048]{1,0:T(8,128)(2,1)}, bf16[352,2048]{1,0:T(8,128)(2,1)}, u32[]{:S(2)}, u32[]{:S(2)}) collective-permute-start(bf16[352,2048]{1,0:T(8,128)(2,1)} %bitcast.69), channel_id=1, source_target_pairs={{0,1},{1,0},{2,3},{3,2},{4,5},{5,4},{6,7},{7,6},{8,9},{9,8},{10,11... | collective-permute-start | bytes 4325384 | tf_op jit(solution)/shard_map/ppermute | solution.py:34
  23.1 2.4 %copy-start.3 = (bf16[512,2048]{1,0:T(8,128)(2,1)S(1)}, bf16[512,2048]{1,0:T(8,128)(2,1)}, u32[]{:S(2)}) copy-start(bf16[512,2048]{1,0:T(8,128)(2,1)} %param.17) | copy-start | bytes 6291460
  23.1 2.4 %copy-start.4 = (bf16[128,2048]{1,0:T(8,128)(2,1)S(1)}, bf16[128,2048]{1,0:T(8,128)(2,1)}, u32[]{:S(2)}) copy-start(bf16[128,2048]{1,0:T(8,128)(2,1)} %param.15) | copy-start | bytes 1572868
  23.6 5.1 %copy-start.5 = (f32[2048]{0:T(1024)S(1)}, f32[2048]{0:T(1024)}, u32[]{:S(2)}) copy-start(f32[2048]{0:T(1024)} %param.18) | copy-start | bytes 24580
  23.6 2.9 %collective-permute-start.2 = (bf16[128,512]{0,1:T(8,128)(2,1)S(1)}, bf16[128,512]{0,1:T(8,128)(2,1)S(1)}, u32[]{:S(2)}, u32[]{:S(2)}) collective-permute-start(bf16[128,512]{0,1:T(8,128)(2,1)S(1)} %constant_dynamic-slice_fusion), channel_id=1, source_target_pairs={{0,1},{1,0},{2,3},{3,2},{4,5},{5,4},{6,7},{7,6},{8,9},{9,8},{10,11... | collective-permute-start | bytes 393224 | tf_op jit(solution)/shard_map/ppermute | solution.py:34
  30.6 79.2 %copy-start.6 = (bf16[1,2048,352]{1,2,0:T(8,128)(2,1)S(1)}, bf16[1,2048,352]{1,2,0:T(8,128)(2,1)}, u32[]{:S(2)}) copy-start(bf16[1,2048,352]{1,2,0:T(8,128)(2,1)} %param.21) | copy-start | bytes 4325380
  109.7 8.8 %copy-start.1 = (bf16[4,4,4,3,8,2048]{5,4,3,2,1,0:T(8,128)(2,1)}, bf16[4,4,4,3,8,2048]{5,4,3,2,1,0:T(8,128)(2,1)S(1)}, u32[]{:S(2)}) copy-start(bf16[4,4,4,3,8,2048]{5,4,3,2,1,0:T(8,128)(2,1)S(1)} %exchange_0.1) | copy-start | bytes 18874372
  137.4 2.8 %copy-start.2 = (bf16[1536,2048]{1,0:T(8,128)(2,1)S(1)}, bf16[1536,2048]{1,0:T(8,128)(2,1)}, u32[]{:S(2)}) copy-start(bf16[1536,2048]{1,0:T(8,128)(2,1)} %convolution_convert_fusion) | copy-start | bytes 18874372

commit v3 on v1

--- a/solution.py
+++ b/solution.py
@@ -3,11 +3,16 @@
 import jax
 import jax.numpy as jnp
 from jax import lax
+from jax.experimental import pallas as pl
+from jax.experimental.pallas import tpu as pltpu
 from jax.sharding import PartitionSpec as P
 
 HD = 128
 TOP = 6
 SWAP = [(0, 1), (1, 0)]
+SIDE = 4
+AXES = ("z", "y", "x")
+ORDERS = ((2, 1, 0), (1, 0, 2), (0, 2, 1))
 
 
 def with_halo(cells, axis, dim, width):
@@ -29,6 +34,284 @@
     return lax.ppermute(block, "exp", SWAP)
 
 
+def peer(axis, delta):
+    me = lax.axis_index("seq")
+    at = [me // (SIDE * SIDE), (me // SIDE) % SIDE, me % SIDE]
+    at[axis] = (at[axis] + delta) % SIDE
+    return ((at[0] * SIDE + at[1]) * SIDE + at[2], lax.axis_index("exp"))
+
+
+def cell(group, **fixed):
+    return tuple(fixed.get(AXES[i], slice(None)) for i in range(3)) + (group,)
+
+
+def tile(group, last, **fixed):
+    c = ORDERS[group][2]
+    rest = tuple(fixed.get(AXES[i], slice(None)) for i in range(3) if i != c)
+    return (last, group) + rest
+
+
+def expert_kernel(
+    src,
+    gate_w,
+    up_w,
+    down_w,
+    out,
+    first,
+    second,
+    arrived,
+    result,
+    third,
+    fourth,
+    weights,
+    rows,
+    act,
+    local_sem,
+    send_sem,
+    recv_sem,
+):
+    mesh_id = pl.DeviceIdType.MESH
+    partner = (lax.axis_index("seq"), 1 - lax.axis_index("exp"))
+    barrier = pltpu.get_barrier_semaphore()
+    for axis in range(3):
+        for delta in range(1, SIDE):
+            pl.semaphore_signal(barrier, inc=1, device_id=peer(axis, delta), device_id_type=mesh_id)
+    pl.semaphore_signal(barrier, inc=1, device_id=partner, device_id_type=mesh_id)
+    pl.semaphore_wait(barrier, 3 * (SIDE - 1) + 1)
+
+    sent = []
+    moved = []
+
+    def send_to(device, source, target):
+        copy = pltpu.make_async_remote_copy(
+            src_ref=source,
+            dst_ref=target,
+            send_sem=send_sem.at[len(sent)],
+            recv_sem=recv_sem.at[len(sent)],
+            device_id=device,
+            device_id_type=mesh_id,
+        )
+        copy.start()
+        sent.append(copy)
+        return copy
+
+    def send(axis, delta, source, target):
+        return send_to(peer(axis, delta), source, target)
+
+    def move(source, target):
+        copy = pltpu.make_async_copy(source, target, local_sem.at[len(moved)])
+        copy.start()
+        moved.append(copy)
+        return copy
+
+    groups = range(3)
+    deltas = (2, 1, 3)
+    inward = (1, 3, 2)
+    name = [[AXES[axis] for axis in order] for order in ORDERS]
+    one, two, three = {}, {}, {}
+    for d in deltas:
+        for g in groups:
+            na = name[g][0]
+            one[g, d] = send(
+                ORDERS[g][0],
+                d,
+                src.at[cell(g, **{na: d})],
+                first.at[cell(g, **{na: SIDE - d})],
+            )
+    swapped = []
+    own = []
+    for i, w in enumerate((gate_w, up_w, down_w)):
+        swapped.append(send_to(partner, w, weights.at[1, i]))
+        own.append(move(w, weights.at[0, i]))
+
+    def relay(i, g, d):
+        na, nb, _ = name[g]
+        held = src if i == 0 else first
+        two[g, i, d] = send(
+            ORDERS[g][1],
+            d,
+            held.at[cell(g, **{na: i, nb: d})],
+            second.at[cell(g, **{na: i, nb: SIDE - d})],
+        )
+
+    def deliver(g, d, held, **at):
+        nc = name[g][2]
+        copy = send(
+            ORDERS[g][2],
+            d,
+            held.at[cell(g, **{nc: d}, **at)],
+            arrived.at[tile(g, SIDE - d, **at)],
+        )
+        three.setdefault(SIDE - d, []).append(copy)
+
+    kept = []
+
+    def keep(g, held, **at):
+        nc = name[g][2]
+        kept.append(move(held.at[cell(g, **{nc: 0}, **at)], arrived.at[tile(g, 0, **at)]))
+
+    for d in deltas:
+        for g in groups:
+            relay(0, g, d)
+    for i in inward:
+        for g in groups:
+            one[g, SIDE - i].wait_recv()
+        for d in deltas:
+            for g in groups:
+                relay(i, g, d)
+    for i in range(SIDE):
+        for d in inward:
+            for g in groups:
+                na, nb, _ = name[g]
+                deliver(g, d, src if i == 0 else first, **{na: i, nb: 0})
+        for g in groups:
+            na, nb, _ = name[g]
+            keep(g, src if i == 0 else first, **{na: i, nb: 0})
+    for j in inward:
+        for i in range(SIDE):
+            for g in groups:
+                two[g, i, SIDE - j].wait_recv()
+        for d in inward:
+            for g in groups:
+                deliver(g, d, second, **{name[g][1]: j})
+        for g in groups:
+            keep(g, second, **{name[g][1]: j})
+
+    for copy in swapped:
+        copy.wait_recv()
+    for copy in own + kept:
+        copy.wait()
+
+    batch = rows.shape[0]
+    width = rows.shape[1]
+    chunk = 512
+    contract = (((1,), (1,)), ((), ()))
+
+    def ffn(j):
+        rows[...] = arrived[j].astype(jnp.float32).reshape(batch, width).astype(jnp.bfloat16)
+
+        @pl.loop(0, 2)
+        def _(h):
+            gate = lax.dot_general(
+                rows[...], weights[h, 0], contract, preferred_element_type=jnp.float32
+            )
+            up = lax.dot_general(
+                rows[...], weights[h, 1], contract, preferred_element_type=jnp.float32
+            )
+            act[h] = (gate / (1.0 + jnp.exp(-gate)) * up).astype(jnp.bfloat16)
+
+        for n in range(0, width, chunk):
+            cols = slice(n, n + chunk)
+            total = jnp.dot(act[0], weights[0, 2, :, cols], preferred_element_type=jnp.float32)
+            total += jnp.dot(act[1], weights[1, 2, :, cols], preferred_element_type=jnp.float32)
+            total = total.reshape(result.shape[1:5] + (chunk,))
+            result[j, :, :, :, :, cols] = total.astype(jnp.bfloat16)
+
+    back_one, back_two, back_three = {}, {}, []
+
+    def back_relay(j, g):
+        held = result if j == 0 else third
+        nb = name[g][1]
+        for d in deltas:
+            back_two[g, j, d] = send(
+                ORDERS[g][1],
+                d,
+                held.at[tile(g, j, **{nb: d})],
+                fourth.at[tile(g, j, **{nb: SIDE - d})],
+            )
+
+    def back_direct(j, g):
+        held = result if j == 0 else third
+        na, nb, nc = name[g]
+        for d in deltas:
+            back_three.append(
+                send(
+                    ORDERS[g][0],
+                    d,
+                    held.at[tile(g, j, **{na: d, nb: 0})],
+                    out.at[cell(g, **{na: SIDE - d, nb: 0, nc: j})],
+                )
+            )
+        move(held.at[tile(g, j, **{na: 0, nb: 0})], out.at[cell(g, **{na: 0, nb: 0, nc: j})])
+
+    for j in (0,) + inward:
+        for copy in three.get(j, ()):
+            copy.wait_recv()
+        ffn(j)
+        for g in groups:
+            if j:
+                back_one[g, j] = send(
+                    ORDERS[g][2], j, result.at[tile(g, j)], third.at[tile(g, SIDE - j)]
+                )
+            else:
+                back_relay(0, g)
+    for g in groups:
+        back_direct(0, g)
+    for j in (3, 1, 2):
+        for g in groups:
+            back_one[g, SIDE - j].wait_recv()
+            back_relay(j, g)
+        for g in groups:
+            back_direct(j, g)
+    for b in inward:
+        for g in groups:
+            for j in range(SIDE):
+                back_two[g, j, SIDE - b].wait_recv()
+        for g in groups:
+            na, nb, _ = name[g]
+            for d in deltas:
+                back_three.append(
+                    send(
+                        ORDERS[g][0],
+                        d,
+                        fourth.at[tile(g, slice(None), **{na: d, nb: b})],
+                        out.at[cell(g, **{na: SIDE - d, nb: b})],
+                    )
+                )
+            move(
+                fourth.at[tile(g, slice(None), **{na: 0, nb: b})],
+                out.at[cell(g, **{na: 0, nb: b})],
+            )
+    for copy in back_three:
+        copy.wait_recv()
+    for copy in moved[len(own) + len(kept) :]:
+        copy.wait()
+    for copy in sent:
+        copy.wait_send()
+
+
+def run_experts(blocks, gate_w, up_w, down_w):
+    dtype = blocks.dtype
+    by_last = (SIDE, 3, SIDE, SIDE) + blocks.shape[4:]
+    batch = 3 * SIDE * SIDE * blocks.shape[4]
+    hidden, width = down_w.shape
+    copies = 2 * 3 * (3 + 4 * 3 + 3 * (4 + 3)) + 3
+    return pl.pallas_call(
+        expert_kernel,
+        out_shape=jax.ShapeDtypeStruct(blocks.shape, dtype),
+        in_specs=[pl.BlockSpec(memory_space=pl.ANY)] * 4,
+        out_specs=pl.BlockSpec(memory_space=pl.ANY),
+        scratch_shapes=[
+            pltpu.VMEM(blocks.shape, dtype),
+            pltpu.VMEM(blocks.shape, dtype),
+            pltpu.VMEM(by_last, dtype),
+            pltpu.VMEM(by_last, dtype),
+            pltpu.VMEM(by_last, dtype),
+            pltpu.VMEM(by_last, dtype),
+            pltpu.VMEM((2, 3, hidden, width), dtype),
+            pltpu.VMEM((batch, width), dtype),
+            pltpu.VMEM((2, batch, hidden), dtype),
+            pltpu.SemaphoreType.DMA((3 + 2 * 3 * (4 + 3),)),
+            pltpu.SemaphoreType.DMA((copies,)),
+            pltpu.SemaphoreType.DMA((copies,)),
+        ],
+        compiler_params=pltpu.CompilerParams(
+            collective_id=0, has_side_effects=True, vmem_limit_bytes=60 << 20
+        ),
+        name="run_experts",
+    )(blocks, gate_w, up_w, down_w)
+
+
 def attention(queries, keys, values, pair_ids):
     tok_rows, local_width = queries.shape
     local_heads = local_width // HD
@@ -58,7 +341,13 @@
 
 def routing(experts, gates, n_experts, capacity):
     rows = experts.shape[0]
-    names = jnp.arange(n_experts, dtype=jnp.int32)
+    step = jnp.arange(n_experts, dtype=jnp.int32)
+    me = lax.axis_index("seq")
+    names = (
+        (step // 16 + me // 16) % SIDE * 16
+        + (step // 4 % SIDE + me // 4 % SIDE) % SIDE * 4
+        + (step % SIDE + me % SIDE) % SIDE
+    )
     hits = experts[:, :, None] == names[None, None, :]
     named = jnp.sum(hits.astype(jnp.float32), axis=1)
     weight = jnp.sum(jnp.where(hits, gates[:, :, None], 0.0), axis=1)
@@ -96,7 +385,6 @@
     mine = lax.dynamic_slice_in_dim(attended, core * moe_rows, moe_rows, 0)
     yours = swap(lax.dynamic_slice_in_dim(attended, (1 - core) * moe_rows, moe_rows, 0))
     out_other = swap(out_weight)
-    gate_other, up_other, down_other = swap(w_gate[0]), swap(w_up[0]), swap(w_down[0])
     stream = (
         resid.astype(jnp.float32)
         + jnp.dot(mine, out_weight, preferred_element_type=jnp.float32)
@@ -106,20 +394,10 @@
     normed = (stream * lax.rsqrt(meansq + 1e-05) * norm_gain).astype(jnp.bfloat16)
     pick, blend = routing(experts, gates, n_experts, capacity)
     outgoing = jnp.dot(pick, normed, preferred_element_type=jnp.float32).astype(jnp.bfloat16)
-    outgoing = outgoing.reshape(n_experts, capacity, normed.shape[1])
-    arrived = lax.all_to_all(outgoing, "seq", split_axis=0, concat_axis=0, tiled=True)
-    inputs = arrived.reshape(n_experts * capacity, arrived.shape[2])
-
-    def half(w_g, w_u, w_d):
-        gate_part = jnp.dot(inputs, w_g, preferred_element_type=jnp.float32)
-        up_part = jnp.dot(inputs, w_u, preferred_element_type=jnp.float32)
-        act = (jax.nn.silu(gate_part) * up_part).astype(jnp.bfloat16)
-        return jnp.dot(act, w_d, preferred_element_type=jnp.float32)
-
-    result = half(w_gate[0], w_up[0], w_down[0]) + half(gate_other, up_other, down_other)
-    result = result.astype(jnp.bfloat16).reshape(n_experts, capacity, arrived.shape[2])
-    back = lax.all_to_all(result, "seq", split_axis=0, concat_axis=0, tiled=True)
-    back = back.reshape(n_experts * capacity, back.shape[2])
+    width = normed.shape[1]
+    cells = (SIDE, SIDE, SIDE, 3, capacity // 3, width)
+    back = run_experts(outgoing.reshape(cells), w_gate[0].T, w_up[0].T, w_down[0])
+    back = back.reshape(n_experts * capacity, width)
     mixture = lax.dot_general(
         blend, back, (((0,), (0,)), ((), ())), preferred_element_type=jnp.float32
     )

time: 259 us -> 193 us (0.75)
  Pallas kernels: 0 us -> 150 us
  blocking collectives: 88.7 us -> 0 us
  waiting for transfers between devices: 82.4 us -> 9.47 us
  matrix products: 49.4 us -> 11.4 us
  starting transfers between devices: 28.3 us -> 9.01 us
    pallas_call x0 -> x1, Pallas kernels: none -> 150 us  [run_experts(): pl.pallas_call(expert_kernel, out_shape=jax.ShapeDtypeStruct(blocks.shape...]
    all_to_all x1 -> x0, blocking collectives: 88.7 us -> none  [shards(): lax.all_to_all(result, 'seq', split_axis=0, concat_axis=0, tiled=True)]
    all_to_all x1 -> x0, waiting for transfers between devices: 77.5 us -> none  [shards(): lax.all_to_all(outgoing, 'seq', split_axis=0, concat_axis=0, tiled=True)]
    dot_general x4 -> x0, matrix products: 40.8 us -> none  [the longest x2 27.1 us: half(): return jnp.dot(act, w_d, preferred_element_type=jnp.float32)]
    all_to_all x1 -> x0, starting transfers between devices: 16.5 us -> none  [shards(): lax.all_to_all(outgoing, 'seq', split_axis=0, concat_axis=0, tiled=True)]
    ppermute x1, waiting for transfers between devices: 0.77 us -> 4.38 us  [with_halo(): lax.ppermute(tail, axis, [(i, (i + 1) % count) for i in range(ends)])]
    dot_general x1, matrix products: 1.89 us -> 4.6 us  [shards(): lax.dot_general(blend, back, (((0,), (0,)), ((), ())), preferred_element_...]
  transfers between devices with their start and end apart: 8 -> 4, of which waited for: 4 -> 3; matrix products, arithmetic and copies ran while one was open for 13% -> 4% of each run, Pallas kernels for 0% -> 0%
where the time goes in v3:
time: 193 us; the launch traced here: 189 us
  Pallas kernels  150 us (78%)
  matrix products  11.4 us (6%)
  waiting for transfers between devices  9.47 us (5%)
  starting transfers between devices  9.01 us (5%)
  other arithmetic  6.08 us (3%)
  local copies, waits for them, and re-layouts  3.24 us (2%)
    pallas_call x1, Pallas kernels, run_experts(): pl.pallas_call(expert_kernel, out_shape=jax.ShapeDtypeStruct(blocks.shape...  150 us
    ppermute x1, starting transfers between devices, with_halo(): lax.ppermute(tail, axis, [(i, (i + 1) % count) for i in range(ends)])  4.75 us
    dot_general x1, matrix products, shards(): lax.dot_general(blend, back, (((0,), (0,)), ((), ())), preferred_element_...  4.6 us
    ppermute x1, waiting for transfers between devices, with_halo(): lax.ppermute(head, axis, [((i + 1) % count, i) for i in range(ends)])  4.59 us
    dot_general x1, matrix products, shards(): jnp.dot(pick, normed, preferred_element_type=jnp.float32)  4.54 us
    ppermute x1, waiting for transfers between devices, with_halo(): lax.ppermute(tail, axis, [(i, (i + 1) % count) for i in range(ends)])  4.38 us
  transfers between devices with their start and end apart: 4, of which 3 were waited for; matrix products, arithmetic and copies ran while one was open for 4% of the time, Pallas kernels for 0%

profile of v3, /device:TPU:1, one launch (start us, length us, event | category | flops | bytes accessed | tf_op | source)
XLA Modules:
  0.0 189.5 jit_solution(13445250644269614503)
XLA Ops:
  0.0 0.0 copy-start
  0.0 1.1 copy.25
  1.1 1.1 copy.26
  2.2 0.8 pad_maximum_fusion.1
  3.1 4.8 %collective-permute-start = (bf16[2,256,512]{1,2,0:T(8,128)(2,1)}, bf16[2,256,512]{1,2,0:T(8,128)(2,1)}, u32[]{:S(2)}, u32[]{:S(2)}) collective-permute-start(bf16[2,256,512]{1,2,0:T(8,128)(2,1)} %pad_maximum_fusion.1), channel_id=1, source_target_pairs={{0,2},{2,4},{4,6},{6,8},{8,10},{10,12},{12,14},{14,16},{16,18},{18... | collective-permute-start | bytes 1572872 | tf_op jit(solution)/shard_map/ppermute | solution.py:25
  7.8 1.3 collective-permute-start.1
  9.1 1.0 collective-permute-start.3
  10.2 0.8 fusion.14
  11.0 0.1 convolution_select_fusion
  11.1 0.1 eq.82
  11.2 0.8 pad_dynamic-slice_fusion
  12.0 0.3 select_convert_fusion
  12.3 0.8 pad_dynamic-slice_fusion.1
  13.1 0.3 fusion.8
  13.3 0.2 select_convert_fusion.1
  13.5 4.4 %collective-permute-done = bf16[2,256,512]{1,2,0:T(8,128)(2,1)} collective-permute-done((bf16[2,256,512]{1,2,0:T(8,128)(2,1)}, bf16[2,256,512]{1,2,0:T(8,128)(2,1)}, u32[]{:S(2)}, u32[]{:S(2)}) %collective-permute-start) | collective-permute-done | bytes 524320 | tf_op jit(solution)/shard_map/ppermute | solution.py:25
  17.9 4.6 %collective-permute-done.1 = bf16[2,256,512]{1,2,0:T(8,128)(2,1)} collective-permute-done((bf16[2,256,512]{1,2,0:T(8,128)(2,1)}, bf16[2,256,512]{1,2,0:T(8,128)(2,1)}, u32[]{:S(2)}, u32[]{:S(2)}) %collective-permute-start.1) | collective-permute-done | bytes 524320 | tf_op jit(solution)/shard_map/ppermute | solution.py:27
  22.5 1.3 pad_maximum_fusion
  23.8 0.1 fusion.32
  23.9 0.0 copy-done
  23.9 0.6 fusion.11
  24.6 1.6 fusion.33
  26.2 0.0 copy-start.1
  26.2 0.0 copy-start.2
  26.2 0.4 fusion.7
  26.7 0.0 copy-start.3
  26.7 1.9 %collective-permute-start.2 = (bf16[128,512]{0,1:T(8,128)(2,1)S(1)}, bf16[128,512]{0,1:T(8,128)(2,1)S(1)}, u32[]{:S(2)}, u32[]{:S(2)}) collective-permute-start(bf16[128,512]{0,1:T(8,128)(2,1)S(1)} %constant_dynamic-slice_fusion), channel_id=1, source_target_pairs={{0,1},{1,0},{2,3},{3,2},{4,5},{5,4},{6,7},{7,6},{8,9},{9,8},{10,11... | collective-permute-start | bytes 393224 | tf_op jit(solution)/shard_map/ppermute | solution.py:34
  28.6 0.0 copy-done.1
  28.6 0.0 copy-done.2
  28.6 0.5 convolution_add_fusion.1
  29.1 0.5 collective-permute-done.2
  29.6 0.0 collective-permute-done.3
  29.6 0.5 multiply_reduce_fusion
  30.2 0.0 copy-done.3
  30.2 4.5 %convolution_convert_fusion = bf16[1536,2048]{1,0:T(8,128)(2,1)} fusion(bf16[1536,128]{1,0:T(8,128)(2,1)S(1)} %select_convert_fusion, f32[128,2048]{1,0:T(8,128)S(1)} %get-tuple-element.12, f32[2048]{0:T(1024)S(1)} %copy-done.3, f32[128]{0:T(128)S(1)} %add_rsqrt_fusion), kind=kOutput, calls=%fused_computation.1 | convolution fusion | flops 809238528 | bytes 7741952 | tf_op jit(solution)/shard_map/dot_general | solution.py:396
  34.7 150.1 %run_experts.1 = bf16[4,4,4,3,8,2048]{5,4,3,2,1,0:T(8,128)(2,1)} custom-call(bf16[4,4,4,3,8,2048]{5,4,3,2,1,0:T(8,128)(2,1)} %bitcast.51, bf16[352,2048]{1,0:T(8,128)(2,1)} %bitcast.58, bf16[352,2048]{1,0:T(8,128)(2,1)} %bitcast.59, bf16[352,2048]{1,0:T(8,128)(2,1)} %bitcast.60), custom_call_target="tpu_custom_call" | custom-call | tf_op jit(solution)/shard_map/run_experts/pallas_call | solution.py:289
  184.9 4.6 %fusion.1 = bf16[128,2048]{1,0:T(8,128)(2,1)} fusion(f32[128,2048]{1,0:T(8,128)S(1)} %get-tuple-element.12, bf16[1536,128]{1,0:T(8,128)(2,1)S(1)} %bitcast.52, bf16[1536,2048]{1,0:T(8,128)(2,1)} %bitcast.50), kind=kOutput, calls=%fused_computation.8 | convolution fusion | flops 805830656 | bytes 8257536 | tf_op jit(solution)/shard_map/dot_general | solution.py:401
  (5 shorter events, 0.0 us)
Async XLA Ops:
  0.0 23.9 %copy-start = (bf16[256,512]{1,0:T(8,128)(2,1)S(1)}, bf16[256,512]{1,0:T(8,128)(2,1)}, u32[]{:S(2)}) copy-start(bf16[256,512]{1,0:T(8,128)(2,1)} %param.12) | copy-start | bytes 786436
  3.1 14.8 %collective-permute-start = (bf16[2,256,512]{1,2,0:T(8,128)(2,1)}, bf16[2,256,512]{1,2,0:T(8,128)(2,1)}, u32[]{:S(2)}, u32[]{:S(2)}) collective-permute-start(bf16[2,256,512]{1,2,0:T(8,128)(2,1)} %pad_maximum_fusion.1), channel_id=1, source_target_pairs={{0,2},{2,4},{4,6},{6,8},{8,10},{10,12},{12,14},{14,16},{16,18},{18... | collective-permute-start | bytes 1572872 | tf_op jit(solution)/shard_map/ppermute | solution.py:25
  7.8 14.7 %collective-permute-start.1 = (bf16[2,256,512]{1,2,0:T(8,128)(2,1)}, bf16[2,256,512]{1,2,0:T(8,128)(2,1)}, u32[]{:S(2)}, u32[]{:S(2)}) collective-permute-start(bf16[2,256,512]{1,2,0:T(8,128)(2,1)} %pad_maximum_fusion.1), channel_id=1, source_target_pairs={{2,0},{4,2},{6,4},{8,6},{10,8},{12,10},{14,12},{16,14},{18,16},{20... | collective-permute-start | bytes 1572872 | tf_op jit(solution)/shard_map/ppermute | solution.py:27
  9.1 20.5 %collective-permute-start.3 = (bf16[512,2048]{1,0:T(8,128)(2,1)}, bf16[512,2048]{1,0:T(8,128)(2,1)S(1)}, u32[]{:S(2)}, u32[]{:S(2)}) collective-permute-start(bf16[512,2048]{1,0:T(8,128)(2,1)} %param.17), channel_id=1, source_target_pairs={{0,1},{1,0},{2,3},{3,2},{4,5},{5,4},{6,7},{7,6},{8,9},{9,8},{10,11... | collective-permute-start | bytes 6291464 | tf_op jit(solution)/shard_map/ppermute | solution.py:34
  26.2 2.4 %copy-start.1 = (bf16[512,2048]{1,0:T(8,128)(2,1)S(1)}, bf16[512,2048]{1,0:T(8,128)(2,1)}, u32[]{:S(2)}) copy-start(bf16[512,2048]{1,0:T(8,128)(2,1)} %param.17) | copy-start | bytes 6291460
  26.2 2.4 %copy-start.2 = (bf16[128,2048]{1,0:T(8,128)(2,1)S(1)}, bf16[128,2048]{1,0:T(8,128)(2,1)}, u32[]{:S(2)}) copy-start(bf16[128,2048]{1,0:T(8,128)(2,1)} %param.15) | copy-start | bytes 1572868
  26.7 3.5 %copy-start.3 = (f32[2048]{0:T(1024)S(1)}, f32[2048]{0:T(1024)}, u32[]{:S(2)}) copy-start(f32[2048]{0:T(1024)} %param.18) | copy-start | bytes 24580
  26.7 2.9 %collective-permute-start.2 = (bf16[128,512]{0,1:T(8,128)(2,1)S(1)}, bf16[128,512]{0,1:T(8,128)(2,1)S(1)}, u32[]{:S(2)}, u32[]{:S(2)}) collective-permute-start(bf16[128,512]{0,1:T(8,128)(2,1)S(1)} %constant_dynamic-slice_fusion), channel_id=1, source_target_pairs={{0,1},{1,0},{2,3},{3,2},{4,5},{5,4},{6,7},{7,6},{8,9},{9,8},{10,11... | collective-permute-start | bytes 393224 | tf_op jit(solution)/shard_map/ppermute | solution.py:34

commit v4 on v3

--- a/solution.py
+++ b/solution.py
@@ -12,6 +12,8 @@
 SWAP = [(0, 1), (1, 0)]
 SIDE = 4
 AXES = ("z", "y", "x")
+SLICES = ((0, 640), (640, 640), (1280, 768))
+FANS = ((2, 1, 0), (1, 0, 2), (0, 2, 1))
 ORDERS = ((2, 1, 0), (1, 0, 2), (0, 2, 1))
 
 
@@ -51,14 +53,59 @@
     return (last, group) + rest
 
 
+def spot(part, last, **fixed):
+    rest = tuple(fixed.get(AXES[i], slice(None)) for i in range(3) if i != FANS[part][2])
+    return (last,) + rest
+
+
+def place(part, **fixed):
+    start, width = SLICES[part]
+    at = tuple(fixed.get(AXES[i], slice(None)) for i in range(3))
+    return at + (slice(None), slice(None), pl.ds(start, width))
+
+
+def picks(names, part):
+    rows = names.shape[1]
+    me = lax.axis_index("seq")
+    here = [me // (SIDE * SIDE), (me // SIDE) % SIDE, me % SIDE]
+    scale = (SIDE * SIDE, SIDE, 1)
+    a, b, c = FANS[part]
+    step = lax.broadcasted_iota(jnp.int32, (SIDE * SIDE, rows), 0)
+    expert = (
+        here[a] * scale[a]
+        + (((step >> 2) + here[b]) & 3) * scale[b]
+        + (((step & 3) + here[c]) & 3) * scale[c]
+    ).astype(jnp.float32)
+    named = jnp.zeros((SIDE * SIDE, rows), jnp.float32)
+    for k in range(TOP):
+        named += jnp.where(names[k : k + 1, :] == expert, 1.0, 0.0)
+    earlier = lax.broadcasted_iota(jnp.int32, (rows, rows), 0)
+    later = lax.broadcasted_iota(jnp.int32, (rows, rows), 1)
+    before = jnp.where(earlier < later, 1.0, 0.0).astype(jnp.bfloat16)
+    ranks = jnp.dot(named.astype(jnp.bfloat16), before, preferred_element_type=jnp.float32)
+    ranks = jnp.where(named > 0.5, ranks, -1.0)
+    slots = lax.broadcasted_iota(jnp.int32, (SIDE * SIDE, 24, rows), 1).astype(jnp.float32)
+    pick = jnp.where(ranks[:, None, :] == slots, 1.0, 0.0)
+    return pick.reshape(SIDE * SIDE * 24, rows).astype(jnp.bfloat16)
+
+
 def expert_kernel(
-    src,
+    normed,
+    names,
     gate_w,
     up_w,
     down_w,
     out,
-    first,
-    second,
+    fan0,
+    fan1,
+    fan2,
+    out0,
+    out1,
+    out2,
+    mid0,
+    mid1,
+    mid2,
+    far_names,
     arrived,
     result,
     third,
@@ -108,15 +155,15 @@
     deltas = (2, 1, 3)
     inward = (1, 3, 2)
     name = [[AXES[axis] for axis in order] for order in ORDERS]
-    one, two, three = {}, {}, {}
+    fans, outs, mids = (fan0, fan1, fan2), (out0, out1, out2), (mid0, mid1, mid2)
+    fan_name = [[AXES[axis] for axis in order] for order in FANS]
+    one, two, three, info = {}, {}, [], {}
     for d in deltas:
-        for g in groups:
-            na = name[g][0]
-            one[g, d] = send(
-                ORDERS[g][0],
-                d,
-                src.at[cell(g, **{na: d})],
-                first.at[cell(g, **{na: SIDE - d})],
+        for f in groups:
+            axis = FANS[f][0]
+            info[f, d] = send(axis, d, names, far_names.at[f, SIDE - d])
+            one[f, d] = send(
+                axis, d, normed.at[:, pl.ds(*SLICES[f])], fans[f].at[SIDE - d]
             )
     swapped = []
     own = []
@@ -124,59 +171,53 @@
         swapped.append(send_to(partner, w, weights.at[1, i]))
         own.append(move(w, weights.at[0, i]))
 
-    def relay(i, g, d):
-        na, nb, _ = name[g]
-        held = src if i == 0 else first
-        two[g, i, d] = send(
-            ORDERS[g][1],
-            d,
-            held.at[cell(g, **{na: i, nb: d})],
-            second.at[cell(g, **{na: i, nb: SIDE - d})],
-        )
-
-    def deliver(g, d, held, **at):
-        nc = name[g][2]
-        copy = send(
-            ORDERS[g][2],
-            d,
-            held.at[cell(g, **{nc: d}, **at)],
-            arrived.at[tile(g, SIDE - d, **at)],
-        )
-        three.setdefault(SIDE - d, []).append(copy)
-
+    def select(f, r):
+        start, wide = SLICES[f]
+        _, nb, _ = fan_name[f]
+        na = fan_name[f][0]
+        table = names[...] if r == 0 else far_names[f, r]
+        tokens = normed[:, start : start + wide] if r == 0 else fans[f][r]
+        chosen = jnp.dot(picks(table, f), tokens, preferred_element_type=jnp.float32)
+        chosen = chosen.reshape(SIDE, SIDE, 3, 8, wide)
+        mids[f][spot(f, slice(None), **{na: r, nb: 0})] = chosen[0].astype(jnp.bfloat16)
+        for d in range(1, SIDE):
+            outs[f][d, :, r] = chosen[d].astype(jnp.bfloat16)
+
+    for r in (0,) + inward:
+        for f in groups:
+            na, nb, _ = fan_name[f]
+            if r:
+                info[f, SIDE - r].wait_recv()
+                one[f, SIDE - r].wait_recv()
+            select(f, r)
+            for d in deltas:
+                two[f, r, d] = send(
+                    FANS[f][1],
+                    d,
+                    outs[f].at[d, :, r],
+                    mids[f].at[spot(f, slice(None), **{na: r, nb: SIDE - d})],
+                )
     kept = []
-
-    def keep(g, held, **at):
-        nc = name[g][2]
-        kept.append(move(held.at[cell(g, **{nc: 0}, **at)], arrived.at[tile(g, 0, **at)]))
-
-    for d in deltas:
-        for g in groups:
-            relay(0, g, d)
-    for i in inward:
-        for g in groups:
-            one[g, SIDE - i].wait_recv()
-        for d in deltas:
-            for g in groups:
-                relay(i, g, d)
-    for i in range(SIDE):
-        for d in inward:
-            for g in groups:
-                na, nb, _ = name[g]
-                deliver(g, d, src if i == 0 else first, **{na: i, nb: 0})
-        for g in groups:
-            na, nb, _ = name[g]
-            keep(g, src if i == 0 else first, **{na: i, nb: 0})
-    for j in inward:
-        for i in range(SIDE):
-            for g in groups:
-                two[g, i, SIDE - j].wait_recv()
-        for d in inward:
-            for g in groups:
-                deliver(g, d, second, **{name[g][1]: j})
-        for g in groups:
-            keep(g, second, **{name[g][1]: j})
-
+    for i in (0,) + inward:
+        for f in groups:
+            _, nb, nc = fan_name[f]
+            if i:
+                for r in range(SIDE):
+                    two[f, r, SIDE - i].wait_recv()
+            for d in deltas:
+                three.append(
+                    send(
+                        FANS[f][2],
+                        d,
+                        mids[f].at[spot(f, d, **{nb: i})],
+                        arrived.at[place(f, **{nb: i, nc: SIDE - d})],
+                    )
+                )
+            kept.append(
+                move(mids[f].at[spot(f, 0, **{nb: i})], arrived.at[place(f, **{nb: i, nc: 0})])
+            )
+    for copy in three:
+        copy.wait_recv()
     for copy in swapped:
         copy.wait_recv()
     for copy in own + kept:
@@ -188,7 +229,10 @@
     contract = (((1,), (1,)), ((), ()))
 
     def ffn(j):
-        rows[...] = arrived[j].astype(jnp.float32).reshape(batch, width).astype(jnp.bfloat16)
+        part = batch // 3
+        for g in groups:
+            block = arrived[cell(g, **{name[g][2]: j})].astype(jnp.float32)
+            rows[g * part : (g + 1) * part, :] = block.reshape(part, width).astype(jnp.bfloat16)
 
         @pl.loop(0, 2)
         def _(h):
@@ -235,8 +279,6 @@
         move(held.at[tile(g, j, **{na: 0, nb: 0})], out.at[cell(g, **{na: 0, nb: 0, nc: j})])
 
     for j in (0,) + inward:
-        for copy in three.get(j, ()):
-            copy.wait_recv()
         ffn(j)
         for g in groups:
             if j:
@@ -280,28 +322,34 @@
         copy.wait_send()
 
 
-def run_experts(blocks, gate_w, up_w, down_w):
-    dtype = blocks.dtype
-    by_last = (SIDE, 3, SIDE, SIDE) + blocks.shape[4:]
-    batch = 3 * SIDE * SIDE * blocks.shape[4]
+def run_experts(normed, names, gate_w, up_w, down_w):
+    dtype = normed.dtype
+    tokens = normed.shape[0]
     hidden, width = down_w.shape
-    copies = 2 * 3 * (3 + 4 * 3 + 3 * (4 + 3)) + 3
+    cells = (SIDE, SIDE, SIDE, 3, 8)
+    by_last = (SIDE, 3, SIDE, SIDE, 8, width)
+    batch = 3 * SIDE * SIDE * 8
+    copies = 3 * (2 * 3 + 4 * 3 + 4 * 3) + 3 + 3 * (3 + 4 * 3 + 3 * (4 + 3))
+    vmem = pl.BlockSpec(memory_space=pltpu.VMEM)
+    hbm = pl.BlockSpec(memory_space=pl.ANY)
     return pl.pallas_call(
         expert_kernel,
-        out_shape=jax.ShapeDtypeStruct(blocks.shape, dtype),
-        in_specs=[pl.BlockSpec(memory_space=pl.ANY)] * 4,
-        out_specs=pl.BlockSpec(memory_space=pl.ANY),
-        scratch_shapes=[
-            pltpu.VMEM(blocks.shape, dtype),
-            pltpu.VMEM(blocks.shape, dtype),
-            pltpu.VMEM(by_last, dtype),
+        out_shape=jax.ShapeDtypeStruct(cells + (width,), dtype),
+        in_specs=[vmem, vmem, hbm, hbm, hbm],
+        out_specs=hbm,
+        scratch_shapes=[pltpu.VMEM((SIDE, tokens, wide), dtype) for _, wide in SLICES]
+        + [pltpu.VMEM(cells + (wide,), dtype) for _, wide in SLICES]
+        + [pltpu.VMEM(cells + (wide,), dtype) for _, wide in SLICES]
+        + [
+            pltpu.VMEM((3, SIDE, 8, tokens), jnp.float32),
+            pltpu.VMEM(cells + (width,), dtype),
             pltpu.VMEM(by_last, dtype),
             pltpu.VMEM(by_last, dtype),
             pltpu.VMEM(by_last, dtype),
             pltpu.VMEM((2, 3, hidden, width), dtype),
             pltpu.VMEM((batch, width), dtype),
             pltpu.VMEM((2, batch, hidden), dtype),
-            pltpu.SemaphoreType.DMA((3 + 2 * 3 * (4 + 3),)),
+            pltpu.SemaphoreType.DMA((3 + 3 * 4 + 3 * (4 + 3),)),
             pltpu.SemaphoreType.DMA((copies,)),
             pltpu.SemaphoreType.DMA((copies,)),
         ],
@@ -309,7 +357,7 @@
             collective_id=0, has_side_effects=True, vmem_limit_bytes=60 << 20
         ),
         name="run_experts",
-    )(blocks, gate_w, up_w, down_w)
+    )(normed, names, gate_w, up_w, down_w)
 
 
 def attention(queries, keys, values, pair_ids):
@@ -357,10 +405,9 @@
     ranks = jnp.where(named > 0.0, ranks, -1.0)
     slots = jnp.arange(capacity, dtype=jnp.int32).astype(jnp.float32)
     chosen = ranks.T[:, None, :] == slots[None, :, None]
-    pick = jnp.where(chosen, 1.0, 0.0).reshape(n_experts * capacity, rows).astype(jnp.bfloat16)
     blend = jnp.where(chosen, weight.T[:, None, :], 0.0)
     blend = blend.reshape(n_experts * capacity, rows).astype(jnp.bfloat16)
-    return pick, blend
+    return blend
 
 
 def shards(
@@ -392,11 +439,10 @@
     )
     meansq = jnp.mean(stream * stream, axis=-1, keepdims=True)
     normed = (stream * lax.rsqrt(meansq + 1e-05) * norm_gain).astype(jnp.bfloat16)
-    pick, blend = routing(experts, gates, n_experts, capacity)
-    outgoing = jnp.dot(pick, normed, preferred_element_type=jnp.float32).astype(jnp.bfloat16)
+    blend = routing(experts, gates, n_experts, capacity)
     width = normed.shape[1]
-    cells = (SIDE, SIDE, SIDE, 3, capacity // 3, width)
-    back = run_experts(outgoing.reshape(cells), w_gate[0].T, w_up[0].T, w_down[0])
+    names = jnp.pad(experts.T.astype(jnp.float32), ((0, 8 - TOP), (0, 0)), constant_values=-1.0)
+    back = run_experts(normed, names, w_gate[0].T, w_up[0].T, w_down[0])
     back = back.reshape(n_experts * capacity, width)
     mixture = lax.dot_general(
         blend, back, (((0,), (0,)), ((), ())), preferred_element_type=jnp.float32

time: 193 us -> 185 us (0.959); the launches traced: 189 us -> 184 us
  matrix products: 11.4 us -> 6.78 us
    dot_general x1 -> x0, matrix products: 4.54 us -> none  [shards(): jnp.dot(pick, normed, preferred_element_type=jnp.float32)]
  transfers between devices with their start and end apart: 4 -> 4, of which waited for: 3 -> 3; matrix products, arithmetic and copies ran while one was open for 4% -> 5% of each run, Pallas kernels for 0% -> 0%
where the time goes in v4:
time: 185 us; the launch traced here: 184 us
  Pallas kernels  149 us (81%)
  starting transfers between devices  9.01 us (5%)
  waiting for transfers between devices  8.58 us (5%)
  other arithmetic  7.44 us (4%)
  matrix products  6.78 us (4%)
  local copies, waits for them, and re-layouts  3.74 us (2%)
    pallas_call x1, Pallas kernels, run_experts(): pl.pallas_call(expert_kernel, out_shape=jax.ShapeDtypeStruct(cells + (wid...  149 us
    ppermute x1, starting transfers between devices, with_halo(): lax.ppermute(tail, axis, [(i, (i + 1) % count) for i in range(ends)])  4.75 us
    dot_general x1, matrix products, shards(): lax.dot_general(blend, back, (((0,), (0,)), ((), ())), preferred_element_...  4.6 us
    ppermute x1, waiting for transfers between devices, with_halo(): lax.ppermute(head, axis, [((i + 1) % count, i) for i in range(ends)])  4.59 us
  transfers between devices with their start and end apart: 4, of which 3 were waited for; matrix products, arithmetic and copies ran while one was open for 5% of the time, Pallas kernels for 0%

profile of v4, /device:TPU:1, one launch (start us, length us, event | category | flops | bytes accessed | tf_op | source)
XLA Modules:
  0.0 184.4 jit_solution(14630373811616368112)
XLA Ops:
  0.0 0.0 copy-start
  0.0 1.1 copy.25
  1.1 1.1 copy.26
  2.2 0.8 pad_maximum_fusion.1
  3.1 4.8 %collective-permute-start = (bf16[2,256,512]{1,2,0:T(8,128)(2,1)}, bf16[2,256,512]{1,2,0:T(8,128)(2,1)}, u32[]{:S(2)}, u32[]{:S(2)}) collective-permute-start(bf16[2,256,512]{1,2,0:T(8,128)(2,1)} %pad_maximum_fusion.1), channel_id=1, source_target_pairs={{0,2},{2,4},{4,6},{6,8},{8,10},{10,12},{12,14},{14,16},{16,18},{18... | collective-permute-start | bytes 1572872 | tf_op jit(solution)/shard_map/ppermute | solution.py:27
  7.8 1.3 collective-permute-start.1
  9.1 1.0 collective-permute-start.3
  10.1 0.8 pad_dynamic-slice_fusion.1
  10.9 0.8 pad_dynamic-slice_fusion
  11.7 0.7 convert_bitcast_fusion
  12.4 0.8 fusion.12
  13.2 0.1 convolution_select_fusion
  13.3 0.6 pad.9.names
  14.0 0.3 fusion.8
  14.2 0.2 select_convert_fusion
  14.4 3.5 %collective-permute-done = bf16[2,256,512]{1,2,0:T(8,128)(2,1)} collective-permute-done((bf16[2,256,512]{1,2,0:T(8,128)(2,1)}, bf16[2,256,512]{1,2,0:T(8,128)(2,1)}, u32[]{:S(2)}, u32[]{:S(2)}) %collective-permute-start) | collective-permute-done | bytes 524320 | tf_op jit(solution)/shard_map/ppermute | solution.py:27
  17.9 4.6 %collective-permute-done.1 = bf16[2,256,512]{1,2,0:T(8,128)(2,1)} collective-permute-done((bf16[2,256,512]{1,2,0:T(8,128)(2,1)}, bf16[2,256,512]{1,2,0:T(8,128)(2,1)}, u32[]{:S(2)}, u32[]{:S(2)}) %collective-permute-start.1) | collective-permute-done | bytes 524320 | tf_op jit(solution)/shard_map/ppermute | solution.py:29
  22.5 1.3 pad_maximum_fusion
  23.8 0.1 fusion.30
  23.9 0.0 copy-done
  23.9 0.6 fusion.9
  24.6 1.6 fusion.31
  26.2 0.0 copy-start.1
  26.2 0.0 copy-start.2
  26.2 0.4 fusion.7
  26.6 0.0 copy-start.3
  26.6 1.9 %collective-permute-start.2 = (bf16[128,512]{0,1:T(8,128)(2,1)S(1)}, bf16[128,512]{0,1:T(8,128)(2,1)S(1)}, u32[]{:S(2)}, u32[]{:S(2)}) collective-permute-start(bf16[128,512]{0,1:T(8,128)(2,1)S(1)} %constant_dynamic-slice_fusion), channel_id=1, source_target_pairs={{0,1},{1,0},{2,3},{3,2},{4,5},{5,4},{6,7},{7,6},{8,9},{9,8},{10,11... | collective-permute-start | bytes 393224 | tf_op jit(solution)/shard_map/ppermute | solution.py:36
  28.6 0.0 copy-done.1
  28.6 0.0 copy-done.2
  28.6 0.5 convolution_add_fusion.1
  29.1 0.5 collective-permute-done.2
  29.6 0.0 collective-permute-done.3
  29.6 0.6 multiply_reduce_fusion
  30.1 0.0 copy-done.3
  30.1 1.0 multiply_convert_fusion.normed
  31.1 148.7 %run_experts.1 = bf16[4,4,4,3,8,2048]{5,4,3,2,1,0:T(8,128)(2,1)} custom-call(bf16[128,2048]{1,0:T(8,128)(2,1)} %multiply_convert_fusion.normed, f32[8,128]{1,0:T(8,128)} %pad.9.names, bf16[352,2048]{1,0:T(8,128)(2,1)} %bitcast.53, bf16[352,2048]{1,0:T(8,128)(2,1)} %bitcast.54, bf16[352,2048]{1,0:T(8,128)(2,1)} %bitcast.55), custom_call_target="tpu_custom_call" | custom-call | tf_op jit(solution)/shard_map/run_experts/pallas_call | solution.py:335
  179.8 4.6 %fusion.1 = bf16[128,2048]{1,0:T(8,128)(2,1)} fusion(f32[128,2048]{1,0:T(8,128)S(1)} %get-tuple-element.12, bf16[1536,128]{1,0:T(8,128)(2,1)S(1)} %bitcast.47, bf16[1536,2048]{1,0:T(8,128)(2,1)} %bitcast.46), kind=kOutput, calls=%fused_computation.7 | convolution fusion | flops 805830656 | bytes 8257536 | tf_op jit(solution)/shard_map/dot_general | solution.py:447
  (4 shorter events, 0.0 us)
Async XLA Ops:
  0.0 23.9 %copy-start = (bf16[256,512]{1,0:T(8,128)(2,1)S(1)}, bf16[256,512]{1,0:T(8,128)(2,1)}, u32[]{:S(2)}) copy-start(bf16[256,512]{1,0:T(8,128)(2,1)} %param.12) | copy-start | bytes 786436
  3.1 14.8 %collective-permute-start = (bf16[2,256,512]{1,2,0:T(8,128)(2,1)}, bf16[2,256,512]{1,2,0:T(8,128)(2,1)}, u32[]{:S(2)}, u32[]{:S(2)}) collective-permute-start(bf16[2,256,512]{1,2,0:T(8,128)(2,1)} %pad_maximum_fusion.1), channel_id=1, source_target_pairs={{0,2},{2,4},{4,6},{6,8},{8,10},{10,12},{12,14},{14,16},{16,18},{18... | collective-permute-start | bytes 1572872 | tf_op jit(solution)/shard_map/ppermute | solution.py:27
  7.8 14.7 %collective-permute-start.1 = (bf16[2,256,512]{1,2,0:T(8,128)(2,1)}, bf16[2,256,512]{1,2,0:T(8,128)(2,1)}, u32[]{:S(2)}, u32[]{:S(2)}) collective-permute-start(bf16[2,256,512]{1,2,0:T(8,128)(2,1)} %pad_maximum_fusion.1), channel_id=1, source_target_pairs={{2,0},{4,2},{6,4},{8,6},{10,8},{12,10},{14,12},{16,14},{18,16},{20... | collective-permute-start | bytes 1572872 | tf_op jit(solution)/shard_map/ppermute | solution.py:29
  9.1 20.5 %collective-permute-start.3 = (bf16[512,2048]{1,0:T(8,128)(2,1)}, bf16[512,2048]{1,0:T(8,128)(2,1)S(1)}, u32[]{:S(2)}, u32[]{:S(2)}) collective-permute-start(bf16[512,2048]{1,0:T(8,128)(2,1)} %param.17), channel_id=1, source_target_pairs={{0,1},{1,0},{2,3},{3,2},{4,5},{5,4},{6,7},{7,6},{8,9},{9,8},{10,11... | collective-permute-start | bytes 6291464 | tf_op jit(solution)/shard_map/ppermute | solution.py:36
  26.2 2.4 %copy-start.1 = (bf16[512,2048]{1,0:T(8,128)(2,1)S(1)}, bf16[512,2048]{1,0:T(8,128)(2,1)}, u32[]{:S(2)}) copy-start(bf16[512,2048]{1,0:T(8,128)(2,1)} %param.17) | copy-start | bytes 6291460
  26.2 2.4 %copy-start.2 = (bf16[128,2048]{1,0:T(8,128)(2,1)S(1)}, bf16[128,2048]{1,0:T(8,128)(2,1)}, u32[]{:S(2)}) copy-start(bf16[128,2048]{1,0:T(8,128)(2,1)} %param.15) | copy-start | bytes 1572868
  26.6 3.5 %copy-start.3 = (f32[2048]{0:T(1024)S(1)}, f32[2048]{0:T(1024)}, u32[]{:S(2)}) copy-start(f32[2048]{0:T(1024)} %param.18) | copy-start | bytes 24580
  26.6 2.9 %collective-permute-start.2 = (bf16[128,512]{0,1:T(8,128)(2,1)S(1)}, bf16[128,512]{0,1:T(8,128)(2,1)S(1)}, u32[]{:S(2)}, u32[]{:S(2)}) collective-permute-start(bf16[128,512]{0,1:T(8,128)(2,1)S(1)} %constant_dynamic-slice_fusion), channel_id=1, source_target_pairs={{0,1},{1,0},{2,3},{3,2},{4,5},{5,4},{6,7},{7,6},{8,9},{9,8},{10,11... | collective-permute-start | bytes 393224 | tf_op jit(solution)/shard_map/ppermute | solution.py:36

commit v5 on v4

--- a/solution.py
+++ b/solution.py
@@ -14,7 +14,6 @@
 AXES = ("z", "y", "x")
 SLICES = ((0, 640), (640, 640), (1280, 768))
 FANS = ((2, 1, 0), (1, 0, 2), (0, 2, 1))
-ORDERS = ((2, 1, 0), (1, 0, 2), (0, 2, 1))
 
 
 def with_halo(cells, axis, dim, width):
@@ -43,16 +42,6 @@
     return ((at[0] * SIDE + at[1]) * SIDE + at[2], lax.axis_index("exp"))
 
 
-def cell(group, **fixed):
-    return tuple(fixed.get(AXES[i], slice(None)) for i in range(3)) + (group,)
-
-
-def tile(group, last, **fixed):
-    c = ORDERS[group][2]
-    rest = tuple(fixed.get(AXES[i], slice(None)) for i in range(3) if i != c)
-    return (last, group) + rest
-
-
 def spot(part, last, **fixed):
     rest = tuple(fixed.get(AXES[i], slice(None)) for i in range(3) if i != FANS[part][2])
     return (last,) + rest
@@ -64,7 +53,7 @@
     return at + (slice(None), slice(None), pl.ds(start, width))
 
 
-def picks(names, part):
+def picks(names, part, blend=False):
     rows = names.shape[1]
     me = lax.axis_index("seq")
     here = [me // (SIDE * SIDE), (me // SIDE) % SIDE, me % SIDE]
@@ -77,21 +66,26 @@
         + (((step & 3) + here[c]) & 3) * scale[c]
     ).astype(jnp.float32)
     named = jnp.zeros((SIDE * SIDE, rows), jnp.float32)
+    weight = jnp.zeros((SIDE * SIDE, rows), jnp.float32)
     for k in range(TOP):
-        named += jnp.where(names[k : k + 1, :] == expert, 1.0, 0.0)
+        hit = names[k : k + 1, :] == expert
+        named += jnp.where(hit, 1.0, 0.0)
+        weight += jnp.where(hit, names[8 + k : 9 + k, :], 0.0)
     earlier = lax.broadcasted_iota(jnp.int32, (rows, rows), 0)
     later = lax.broadcasted_iota(jnp.int32, (rows, rows), 1)
     before = jnp.where(earlier < later, 1.0, 0.0).astype(jnp.bfloat16)
     ranks = jnp.dot(named.astype(jnp.bfloat16), before, preferred_element_type=jnp.float32)
     ranks = jnp.where(named > 0.5, ranks, -1.0)
     slots = lax.broadcasted_iota(jnp.int32, (SIDE * SIDE, 24, rows), 1).astype(jnp.float32)
-    pick = jnp.where(ranks[:, None, :] == slots, 1.0, 0.0)
+    chosen = ranks[:, None, :] == slots
+    pick = jnp.where(chosen, weight[:, None, :] if blend else 1.0, 0.0)
     return pick.reshape(SIDE * SIDE * 24, rows).astype(jnp.bfloat16)
 
 
 def expert_kernel(
     normed,
     names,
+    stream,
     gate_w,
     up_w,
     down_w,
@@ -108,8 +102,18 @@
     far_names,
     arrived,
     result,
-    third,
-    fourth,
+    ret0,
+    ret1,
+    ret2,
+    home0,
+    home1,
+    home2,
+    part0,
+    part1,
+    part2,
+    got0,
+    got1,
+    got2,
     weights,
     rows,
     act,
@@ -154,7 +158,6 @@
     groups = range(3)
     deltas = (2, 1, 3)
     inward = (1, 3, 2)
-    name = [[AXES[axis] for axis in order] for order in ORDERS]
     fans, outs, mids = (fan0, fan1, fan2), (out0, out1, out2), (mid0, mid1, mid2)
     fan_name = [[AXES[axis] for axis in order] for order in FANS]
     one, two, three, info = {}, {}, [], {}
@@ -229,10 +232,7 @@
     contract = (((1,), (1,)), ((), ()))
 
     def ffn(j):
-        part = batch // 3
-        for g in groups:
-            block = arrived[cell(g, **{name[g][2]: j})].astype(jnp.float32)
-            rows[g * part : (g + 1) * part, :] = block.reshape(part, width).astype(jnp.bfloat16)
+        rows[...] = arrived[j].astype(jnp.float32).reshape(batch, width).astype(jnp.bfloat16)
 
         @pl.loop(0, 2)
         def _(h):
@@ -251,105 +251,117 @@
             total = total.reshape(result.shape[1:5] + (chunk,))
             result[j, :, :, :, :, cols] = total.astype(jnp.bfloat16)
 
-    back_one, back_two, back_three = {}, {}, []
-
-    def back_relay(j, g):
-        held = result if j == 0 else third
-        nb = name[g][1]
-        for d in deltas:
-            back_two[g, j, d] = send(
-                ORDERS[g][1],
-                d,
-                held.at[tile(g, j, **{nb: d})],
-                fourth.at[tile(g, j, **{nb: SIDE - d})],
-            )
-
-    def back_direct(j, g):
-        held = result if j == 0 else third
-        na, nb, nc = name[g]
-        for d in deltas:
-            back_three.append(
-                send(
-                    ORDERS[g][0],
-                    d,
-                    held.at[tile(g, j, **{na: d, nb: 0})],
-                    out.at[cell(g, **{na: SIDE - d, nb: 0, nc: j})],
-                )
-            )
-        move(held.at[tile(g, j, **{na: 0, nb: 0})], out.at[cell(g, **{na: 0, nb: 0, nc: j})])
-
+    rets, homes = (ret0, ret1, ret2), (home0, home1, home2)
+    parts, gots = (part0, part1, part2), (got0, got1, got2)
+    back_one, back_two, back_three, stay, home = {}, {}, {}, {}, {}
     for j in (0,) + inward:
         ffn(j)
-        for g in groups:
+        for f in groups:
+            axis = FANS[f][2]
+            for d in (0,) + deltas:
+                at = {"z": j}
+                if axis == 0 and d != j:
+                    continue
+                if axis:
+                    at[AXES[axis]] = d
+                rest = {} if axis == 0 else {"z": j}
+                source = result.at[place(f, **at)]
+                if d:
+                    back_one.setdefault((f, SIDE - d), []).append(
+                        send(axis, d, source, rets[f].at[spot(f, SIDE - d, **rest)])
+                    )
+                else:
+                    stay.setdefault(f, []).append(
+                        move(source, rets[f].at[spot(f, 0, **rest)])
+                    )
+    for j in (0,) + inward:
+        for f in groups:
+            nb = fan_name[f][1]
             if j:
-                back_one[g, j] = send(
-                    ORDERS[g][2], j, result.at[tile(g, j)], third.at[tile(g, SIDE - j)]
-                )
+                for copy in back_one[f, j]:
+                    copy.wait_recv()
             else:
-                back_relay(0, g)
-    for g in groups:
-        back_direct(0, g)
-    for j in (3, 1, 2):
-        for g in groups:
-            back_one[g, SIDE - j].wait_recv()
-            back_relay(j, g)
-        for g in groups:
-            back_direct(j, g)
-    for b in inward:
-        for g in groups:
-            for j in range(SIDE):
-                back_two[g, j, SIDE - b].wait_recv()
-        for g in groups:
-            na, nb, _ = name[g]
+                for copy in stay[f]:
+                    copy.wait()
             for d in deltas:
-                back_three.append(
+                back_two.setdefault((f, SIDE - d), []).append(
                     send(
-                        ORDERS[g][0],
+                        FANS[f][1],
                         d,
-                        fourth.at[tile(g, slice(None), **{na: d, nb: b})],
-                        out.at[cell(g, **{na: SIDE - d, nb: b})],
+                        rets[f].at[spot(f, j, **{nb: d})],
+                        homes[f].at[SIDE - d, j],
                     )
                 )
-            move(
-                fourth.at[tile(g, slice(None), **{na: 0, nb: b})],
-                out.at[cell(g, **{na: 0, nb: b})],
-            )
-    for copy in back_three:
-        copy.wait_recv()
-    for copy in moved[len(own) + len(kept) :]:
-        copy.wait()
+            home.setdefault(f, []).append(
+                move(rets[f].at[spot(f, j, **{nb: 0})], homes[f].at[0, j])
+            )
+
+    def blended(f, r):
+        wide = SLICES[f][1]
+        table = names[...] if r == 0 else far_names[f, r]
+        held = homes[f][:, :, r].astype(jnp.float32)
+        held = held.reshape(SIDE * SIDE * 24, wide).astype(jnp.bfloat16)
+        return lax.dot_general(
+            picks(table, f, True),
+            held,
+            (((0,), (0,)), ((), ())),
+            preferred_element_type=jnp.float32,
+        )
+
+    for f in groups:
+        for i in range(1, SIDE):
+            for copy in back_two[f, i]:
+                copy.wait_recv()
+        for copy in home[f]:
+            copy.wait()
+        for r in deltas:
+            parts[f][r] = blended(f, r).astype(jnp.bfloat16)
+        for r in deltas:
+            back_three[f, SIDE - r] = send(
+                FANS[f][0], r, parts[f].at[r], gots[f].at[SIDE - r]
+            )
+    for f in groups:
+        start, wide = SLICES[f]
+        total = stream[:, start : start + wide] + blended(f, 0)
+        for r in range(1, SIDE):
+            back_three[f, r].wait_recv()
+            total += gots[f][r].astype(jnp.float32)
+        out[:, start : start + wide] = total.astype(out.dtype)
     for copy in sent:
         copy.wait_send()
 
 
-def run_experts(normed, names, gate_w, up_w, down_w):
+def run_experts(normed, names, stream, gate_w, up_w, down_w):
     dtype = normed.dtype
     tokens = normed.shape[0]
     hidden, width = down_w.shape
     cells = (SIDE, SIDE, SIDE, 3, 8)
-    by_last = (SIDE, 3, SIDE, SIDE, 8, width)
     batch = 3 * SIDE * SIDE * 8
-    copies = 3 * (2 * 3 + 4 * 3 + 4 * 3) + 3 + 3 * (3 + 4 * 3 + 3 * (4 + 3))
+    copies = 3 * (2 * 3 + 4 * 3 + 4 * 3) + 3 + (3 + 2 * 4 * 3) + 3 * (4 * 3 + 3)
     vmem = pl.BlockSpec(memory_space=pltpu.VMEM)
     hbm = pl.BlockSpec(memory_space=pl.ANY)
     return pl.pallas_call(
         expert_kernel,
-        out_shape=jax.ShapeDtypeStruct(cells + (width,), dtype),
-        in_specs=[vmem, vmem, hbm, hbm, hbm],
-        out_specs=hbm,
+        out_shape=jax.ShapeDtypeStruct((tokens, width), dtype),
+        in_specs=[vmem, vmem, vmem, hbm, hbm, hbm],
+        out_specs=vmem,
         scratch_shapes=[pltpu.VMEM((SIDE, tokens, wide), dtype) for _, wide in SLICES]
         + [pltpu.VMEM(cells + (wide,), dtype) for _, wide in SLICES]
         + [pltpu.VMEM(cells + (wide,), dtype) for _, wide in SLICES]
         + [
-            pltpu.VMEM((3, SIDE, 8, tokens), jnp.float32),
+            pltpu.VMEM((3, SIDE, 16, tokens), jnp.float32),
             pltpu.VMEM(cells + (width,), dtype),
-            pltpu.VMEM(by_last, dtype),
-            pltpu.VMEM(by_last, dtype),
-            pltpu.VMEM(by_last, dtype),
+            pltpu.VMEM(cells + (width,), dtype),
+        ]
+        + [pltpu.VMEM(cells + (wide,), dtype) for _, wide in SLICES]
+        + [pltpu.VMEM(cells + (wide,), dtype) for _, wide in SLICES]
+        + [pltpu.VMEM((SIDE, tokens, wide), dtype) for _, wide in SLICES]
+        + [pltpu.VMEM((SIDE, tokens, wide), dtype) for _, wide in SLICES]
+        + [
             pltpu.VMEM((2, 3, hidden, width), dtype),
             pltpu.VMEM((batch, width), dtype),
             pltpu.VMEM((2, batch, hidden), dtype),
-            pltpu.SemaphoreType.DMA((3 + 3 * 4 + 3 * (4 + 3),)),
+            pltpu.SemaphoreType.DMA((3 + 3 * 4 + (1 + 2 * 4) + 3 * 4,)),
             pltpu.SemaphoreType.DMA((copies,)),
             pltpu.SemaphoreType.DMA((copies,)),
         ],
@@ -357,7 +369,7 @@
             collective_id=0, has_side_effects=True, vmem_limit_bytes=60 << 20
         ),
         name="run_experts",
-    )(normed, names, gate_w, up_w, down_w)
+    )(normed, names, stream, gate_w, up_w, down_w)
 
 
 def attention(queries, keys, values, pair_ids):
@@ -387,29 +399,6 @@
     return attended.reshape(tok_rows, local_width).astype(jnp.bfloat16)
 
 
-def routing(experts, gates, n_experts, capacity):
-    rows = experts.shape[0]
-    step = jnp.arange(n_experts, dtype=jnp.int32)
-    me = lax.axis_index("seq")
-    names = (
-        (step // 16 + me // 16) % SIDE * 16
-        + (step // 4 % SIDE + me // 4 % SIDE) % SIDE * 4
-        + (step % SIDE + me % SIDE) % SIDE
-    )
-    hits = experts[:, :, None] == names[None, None, :]
-    named = jnp.sum(hits.astype(jnp.float32), axis=1)
-    weight = jnp.sum(jnp.where(hits, gates[:, :, None], 0.0), axis=1)
-    order = jnp.arange(rows, dtype=jnp.int32)
-    before = (order[None, :] < order[:, None]).astype(jnp.bfloat16)
-    ranks = jnp.dot(before, named.astype(jnp.bfloat16), preferred_element_type=jnp.float32)
-    ranks = jnp.where(named > 0.0, ranks, -1.0)
-    slots = jnp.arange(capacity, dtype=jnp.int32).astype(jnp.float32)
-    chosen = ranks.T[:, None, :] == slots[None, :, None]
-    blend = jnp.where(chosen, weight.T[:, None, :], 0.0)
-    blend = blend.reshape(n_experts * capacity, rows).astype(jnp.bfloat16)
-    return blend
-
-
 def shards(
     queries,
     keys,
@@ -425,8 +414,6 @@
     w_down,
 ):
     moe_rows = resid.shape[0]
-    n_experts = lax.axis_size("seq") * w_gate.shape[0]
-    capacity = 2 * moe_rows * TOP // n_experts
     core = lax.axis_index("exp")
     attended = attention(queries, keys, values, pair_ids)
     mine = lax.dynamic_slice_in_dim(attended, core * moe_rows, moe_rows, 0)
@@ -439,15 +426,14 @@
     )
     meansq = jnp.mean(stream * stream, axis=-1, keepdims=True)
     normed = (stream * lax.rsqrt(meansq + 1e-05) * norm_gain).astype(jnp.bfloat16)
-    blend = routing(experts, gates, n_experts, capacity)
-    width = normed.shape[1]
-    names = jnp.pad(experts.T.astype(jnp.float32), ((0, 8 - TOP), (0, 0)), constant_values=-1.0)
-    back = run_experts(normed, names, w_gate[0].T, w_up[0].T, w_down[0])
-    back = back.reshape(n_experts * capacity, width)
-    mixture = lax.dot_general(
-        blend, back, (((0,), (0,)), ((), ())), preferred_element_type=jnp.float32
+    lines = ((0, 8 - TOP), (0, 0))
+    names = jnp.concatenate(
+        [
+            jnp.pad(experts.T.astype(jnp.float32), lines, constant_values=-1.0),
+            jnp.pad(gates.T, lines),
+        ]
     )
-    return (stream + mixture).astype(jnp.bfloat16)
+    return run_experts(normed, names, stream, w_gate[0].T, w_up[0].T, w_down[0])
 
 
 def solution(mesh):

time: 185 us -> 175 us (0.946)
  Pallas kernels: 149 us -> 144 us
  matrix products: 6.78 us -> 2.04 us
  waiting for transfers between devices: 8.58 us -> 4.6 us
    dot_general x2 -> x0, matrix products: 4.73 us -> none  [the longest x1 4.6 us: shards(): lax.dot_general(blend, back, (((0,), (0,)), ((), ())), preferred_element_...]
    pallas_call x1, Pallas kernels: 149 us -> 144 us  [run_experts(): pl.pallas_call(expert_kernel, out_shape=jax.ShapeDtypeStruct((tokens, wid...]
    ppermute x1, waiting for transfers between devices: 3.49 us -> 0.77 us  [with_halo(): lax.ppermute(tail, axis, [(i, (i + 1) % count) for i in range(ends)])]
    unnamed x10 -> x13, local copies, waits for them, and re-layouts: 2.23 us -> 4.19 us
where the time goes in v5:
time: 175 us; the launch traced here: 173 us
  Pallas kernels  144 us (82%)
  starting transfers between devices  10.2 us (6%)
  other arithmetic  7.06 us (4%)
  local copies, waits for them, and re-layouts  5.08 us (3%)
  waiting for transfers between devices  4.6 us (3%)
  matrix products  2.04 us (1%)
    pallas_call x1, Pallas kernels, run_experts(): pl.pallas_call(expert_kernel, out_shape=jax.ShapeDtypeStruct((tokens, wid...  144 us
    ppermute x1, starting transfers between devices, with_halo(): lax.ppermute(tail, axis, [(i, (i + 1) % count) for i in range(ends)])  5.38 us
    unnamed x13, local copies, waits for them, and re-layouts  4.19 us
    ppermute x2, starting transfers between devices, swap(): return lax.ppermute(block, 'exp', SWAP)  3.51 us
  transfers between devices with their start and end apart: 4, of which 3 were waited for; matrix products, arithmetic and copies ran while one was open for 5% of the time, Pallas kernels for 0%

profile of v5, /device:TPU:1, one launch (start us, length us, event | category | flops | bytes accessed | tf_op | source)
XLA Modules:
  0.0 173.2 jit_solution(2715524262784847742)
XLA Ops:
  0.0 0.0 copy-start
  0.0 1.1 copy.17
  1.1 1.1 copy.16
  2.2 0.1 pad_maximum_fusion.1
  2.3 1.3 collective-permute-start.1
  3.6 5.4 %collective-permute-start = (bf16[2,256,512]{1,2,0:T(8,128)(2,1)S(1)}, bf16[2,256,512]{1,2,0:T(8,128)(2,1)}, u32[]{:S(2)}, u32[]{:S(2)}) collective-permute-start(bf16[2,256,512]{1,2,0:T(8,128)(2,1)S(1)} %pad_maximum_fusion.1), channel_id=1, source_target_pairs={{0,2},{2,4},{4,6},{6,8},{8,10},{10,12},{12,14},{14,16},{16,18},{18... | collective-permute-start | bytes 1572872 | tf_op jit(solution)/shard_map/ppermute | solution.py:26
  9.0 1.4 collective-permute-start.3
  10.4 0.8 pad_dynamic-slice_fusion.1
  11.1 0.8 pad_dynamic-slice_fusion
  11.9 0.7 convert_bitcast_fusion
  12.6 1.3 select_maximum_fusion.names
  13.9 0.3 fusion.7
  14.2 3.3 %collective-permute-done.1 = bf16[2,256,512]{1,2,0:T(8,128)(2,1)} collective-permute-done((bf16[2,256,512]{1,2,0:T(8,128)(2,1)S(1)}, bf16[2,256,512]{1,2,0:T(8,128)(2,1)}, u32[]{:S(2)}, u32[]{:S(2)}) %collective-permute-start.1) | collective-permute-done | bytes 524320 | tf_op jit(solution)/shard_map/ppermute | solution.py:28
  17.5 0.8 collective-permute-done
  18.2 1.3 pad_maximum_fusion
  19.6 0.1 fusion.15
  19.7 0.0 copy-done
  19.7 0.6 fusion.8
  20.3 1.6 fusion.16
  21.9 0.0 copy-start.2
  21.9 0.0 copy-start.3
  21.9 0.4 fusion.6
  22.4 0.0 copy-start.4
  22.4 2.1 %collective-permute-start.2 = (bf16[128,512]{0,1:T(8,128)(2,1)S(1)}, bf16[128,512]{0,1:T(8,128)(2,1)S(1)}, u32[]{:S(2)}, u32[]{:S(2)}) collective-permute-start(bf16[128,512]{0,1:T(8,128)(2,1)S(1)} %constant_dynamic-slice_fusion), channel_id=1, source_target_pairs={{0,1},{1,0},{2,3},{3,2},{4,5},{5,4},{6,7},{7,6},{8,9},{9,8},{10,11... | collective-permute-start | bytes 393224 | tf_op jit(solution)/shard_map/ppermute | solution.py:35
  24.5 0.0 copy-done.2
  24.5 0.0 copy-done.3
  24.5 0.5 convolution_add_fusion.1
  25.0 0.5 collective-permute-done.2
  25.5 0.0 collective-permute-done.3
  25.5 0.6 multiply_reduce_fusion
  26.0 0.0 copy-start.1
  26.1 0.0 copy-done.4
  26.1 1.1 multiply_convert_fusion.normed
  27.1 0.1 copy-done.1
  27.2 144.0 %run_experts.1 = bf16[128,2048]{1,0:T(8,128)(2,1)} custom-call(bf16[128,2048]{1,0:T(8,128)(2,1)} %multiply_convert_fusion.normed, f32[16,128]{1,0:T(8,128)} %select_maximum_fusion.names, f32[128,2048]{1,0:T(8,128)} %copy-done.1, bf16[352,2048]{1,0:T(8,128)(2,1)} %bitcast.45, bf16[352,2048]{1,0:T(8,128)(2,1)} %bitcast.46, bf16[352,2048]{1,0:T(8,128)(2,1)} %bitcast.47), custom_call_target="tpu_custom_call" | custom-call | tf_op jit(solution)/shard_map/run_experts/pallas_call | solution.py:343
  171.3 1.9 %copy.29 = bf16[128,2048]{1,0:T(8,128)(2,1)} copy(bf16[128,2048]{1,0:T(8,128)(2,1)} %run_experts.1) | data formatting | bytes 1048576
  (2 shorter events, 0.0 us)
Async XLA Ops:
  0.0 19.7 %copy-start = (bf16[256,512]{1,0:T(8,128)(2,1)S(1)}, bf16[256,512]{1,0:T(8,128)(2,1)}, u32[]{:S(2)}) copy-start(bf16[256,512]{1,0:T(8,128)(2,1)} %param.12) | copy-start | bytes 786436
  2.3 15.2 %collective-permute-start.1 = (bf16[2,256,512]{1,2,0:T(8,128)(2,1)S(1)}, bf16[2,256,512]{1,2,0:T(8,128)(2,1)}, u32[]{:S(2)}, u32[]{:S(2)}) collective-permute-start(bf16[2,256,512]{1,2,0:T(8,128)(2,1)S(1)} %pad_maximum_fusion.1), channel_id=1, source_target_pairs={{2,0},{4,2},{6,4},{8,6},{10,8},{12,10},{14,12},{16,14},{18,16},{20... | collective-permute-start | bytes 1572872 | tf_op jit(solution)/shard_map/ppermute | solution.py:28
  3.6 14.7 %collective-permute-start = (bf16[2,256,512]{1,2,0:T(8,128)(2,1)S(1)}, bf16[2,256,512]{1,2,0:T(8,128)(2,1)}, u32[]{:S(2)}, u32[]{:S(2)}) collective-permute-start(bf16[2,256,512]{1,2,0:T(8,128)(2,1)S(1)} %pad_maximum_fusion.1), channel_id=1, source_target_pairs={{0,2},{2,4},{4,6},{6,8},{8,10},{10,12},{12,14},{14,16},{16,18},{18... | collective-permute-start | bytes 1572872 | tf_op jit(solution)/shard_map/ppermute | solution.py:26
  9.0 16.5 %collective-permute-start.3 = (bf16[512,2048]{1,0:T(8,128)(2,1)}, bf16[512,2048]{1,0:T(8,128)(2,1)S(1)}, u32[]{:S(2)}, u32[]{:S(2)}) collective-permute-start(bf16[512,2048]{1,0:T(8,128)(2,1)} %param.17), channel_id=1, source_target_pairs={{0,1},{1,0},{2,3},{3,2},{4,5},{5,4},{6,7},{7,6},{8,9},{9,8},{10,11... | collective-permute-start | bytes 6291464 | tf_op jit(solution)/shard_map/ppermute | solution.py:35
  21.9 2.6 %copy-start.2 = (bf16[512,2048]{1,0:T(8,128)(2,1)S(1)}, bf16[512,2048]{1,0:T(8,128)(2,1)}, u32[]{:S(2)}) copy-start(bf16[512,2048]{1,0:T(8,128)(2,1)} %param.17) | copy-start | bytes 6291460
  21.9 2.6 %copy-start.3 = (bf16[128,2048]{1,0:T(8,128)(2,1)S(1)}, bf16[128,2048]{1,0:T(8,128)(2,1)}, u32[]{:S(2)}) copy-start(bf16[128,2048]{1,0:T(8,128)(2,1)} %param.15) | copy-start | bytes 1572868
  22.4 3.7 %copy-start.4 = (f32[2048]{0:T(1024)S(1)}, f32[2048]{0:T(1024)}, u32[]{:S(2)}) copy-start(f32[2048]{0:T(1024)} %param.18) | copy-start | bytes 24580
  22.4 3.1 %collective-permute-start.2 = (bf16[128,512]{0,1:T(8,128)(2,1)S(1)}, bf16[128,512]{0,1:T(8,128)(2,1)S(1)}, u32[]{:S(2)}, u32[]{:S(2)}) collective-permute-start(bf16[128,512]{0,1:T(8,128)(2,1)S(1)} %constant_dynamic-slice_fusion), channel_id=1, source_target_pairs={{0,1},{1,0},{2,3},{3,2},{4,5},{5,4},{6,7},{7,6},{8,9},{9,8},{10,11... | collective-permute-start | bytes 393224 | tf_op jit(solution)/shard_map/ppermute | solution.py:35
  26.0 1.2 copy-start.1

commit v6 on v5

--- a/solution.py
+++ b/solution.py
@@ -254,7 +254,7 @@
     rets, homes = (ret0, ret1, ret2), (home0, home1, home2)
     parts, gots = (part0, part1, part2), (got0, got1, got2)
     back_one, back_two, back_three, stay, home = {}, {}, {}, {}, {}
-    for j in (0,) + inward:
+    for j in (2, 1, 3, 0):
         ffn(j)
         for f in groups:
             axis = FANS[f][2]

time: 175 us -> 172 us (0.983)
  no operation moved by 1% of the time
where the time goes in v6:
time: 172 us
  Pallas kernels  143 us (83%)
  starting transfers between devices  10.2 us (6%)
  other arithmetic  7.06 us (4%)
  local copies, waits for them, and re-layouts  5.08 us (3%)
  waiting for transfers between devices  4.6 us (3%)
  matrix products  2.04 us (1%)
    pallas_call x1, Pallas kernels, run_experts(): pl.pallas_call(expert_kernel, out_shape=jax.ShapeDtypeStruct((tokens, wid...  143 us
    ppermute x1, starting transfers between devices, with_halo(): lax.ppermute(tail, axis, [(i, (i + 1) % count) for i in range(ends)])  5.38 us
    unnamed x13, local copies, waits for them, and re-layouts  4.19 us
    ppermute x2, starting transfers between devices, swap(): return lax.ppermute(block, 'exp', SWAP)  3.51 us
  transfers between devices with their start and end apart: 4, of which 3 were waited for; matrix products, arithmetic and copies ran while one was open for 5% of the time, Pallas kernels for 0%

profile of v6, /device:TPU:1, one launch (start us, length us, event | category | flops | bytes accessed | tf_op | source)
XLA Modules:
  0.0 171.9 jit_solution(13027569306084931815)
XLA Ops:
  0.0 0.0 copy-start
  0.0 1.1 copy.17
  1.1 1.1 copy.16
  2.2 0.1 pad_maximum_fusion.1
  2.3 1.3 collective-permute-start.1
  3.6 5.4 %collective-permute-start = (bf16[2,256,512]{1,2,0:T(8,128)(2,1)S(1)}, bf16[2,256,512]{1,2,0:T(8,128)(2,1)}, u32[]{:S(2)}, u32[]{:S(2)}) collective-permute-start(bf16[2,256,512]{1,2,0:T(8,128)(2,1)S(1)} %pad_maximum_fusion.1), channel_id=1, source_target_pairs={{0,2},{2,4},{4,6},{6,8},{8,10},{10,12},{12,14},{14,16},{16,18},{18... | collective-permute-start | bytes 1572872 | tf_op jit(solution)/shard_map/ppermute | solution.py:26
  9.0 1.4 collective-permute-start.3
  10.4 0.8 pad_dynamic-slice_fusion.1
  11.1 0.8 pad_dynamic-slice_fusion
  11.9 0.7 convert_bitcast_fusion
  12.6 1.3 select_maximum_fusion.names
  13.9 0.3 fusion.7
  14.2 3.3 %collective-permute-done.1 = bf16[2,256,512]{1,2,0:T(8,128)(2,1)} collective-permute-done((bf16[2,256,512]{1,2,0:T(8,128)(2,1)S(1)}, bf16[2,256,512]{1,2,0:T(8,128)(2,1)}, u32[]{:S(2)}, u32[]{:S(2)}) %collective-permute-start.1) | collective-permute-done | bytes 524320 | tf_op jit(solution)/shard_map/ppermute | solution.py:28
  17.5 0.8 collective-permute-done
  18.2 1.3 pad_maximum_fusion
  19.6 0.1 fusion.15
  19.7 0.0 copy-done
  19.7 0.6 fusion.8
  20.3 1.6 fusion.16
  21.9 0.0 copy-start.2
  21.9 0.0 copy-start.3
  21.9 0.4 fusion.6
  22.4 0.0 copy-start.4
  22.4 2.1 %collective-permute-start.2 = (bf16[128,512]{0,1:T(8,128)(2,1)S(1)}, bf16[128,512]{0,1:T(8,128)(2,1)S(1)}, u32[]{:S(2)}, u32[]{:S(2)}) collective-permute-start(bf16[128,512]{0,1:T(8,128)(2,1)S(1)} %constant_dynamic-slice_fusion), channel_id=1, source_target_pairs={{0,1},{1,0},{2,3},{3,2},{4,5},{5,4},{6,7},{7,6},{8,9},{9,8},{10,11... | collective-permute-start | bytes 393224 | tf_op jit(solution)/shard_map/ppermute | solution.py:35
  24.5 0.0 copy-done.2
  24.5 0.0 copy-done.3
  24.5 0.5 convolution_add_fusion.1
  25.0 0.5 collective-permute-done.2
  25.5 0.0 collective-permute-done.3
  25.5 0.6 multiply_reduce_fusion
  26.0 0.0 copy-start.1
  26.1 0.0 copy-done.4
  26.1 1.1 multiply_convert_fusion.normed
  27.1 0.1 copy-done.1
  27.2 142.8 %run_experts.1 = bf16[128,2048]{1,0:T(8,128)(2,1)} custom-call(bf16[128,2048]{1,0:T(8,128)(2,1)} %multiply_convert_fusion.normed, f32[16,128]{1,0:T(8,128)} %select_maximum_fusion.names, f32[128,2048]{1,0:T(8,128)} %copy-done.1, bf16[352,2048]{1,0:T(8,128)(2,1)} %bitcast.45, bf16[352,2048]{1,0:T(8,128)(2,1)} %bitcast.46, bf16[352,2048]{1,0:T(8,128)(2,1)} %bitcast.47), custom_call_target="tpu_custom_call" | custom-call | tf_op jit(solution)/shard_map/run_experts/pallas_call | solution.py:343
  170.0 1.9 %copy.29 = bf16[128,2048]{1,0:T(8,128)(2,1)} copy(bf16[128,2048]{1,0:T(8,128)(2,1)} %run_experts.1) | data formatting | bytes 1048576
  (2 shorter events, 0.0 us)
Async XLA Ops:
  0.0 19.7 %copy-start = (bf16[256,512]{1,0:T(8,128)(2,1)S(1)}, bf16[256,512]{1,0:T(8,128)(2,1)}, u32[]{:S(2)}) copy-start(bf16[256,512]{1,0:T(8,128)(2,1)} %param.12) | copy-start | bytes 786436
  2.3 15.2 %collective-permute-start.1 = (bf16[2,256,512]{1,2,0:T(8,128)(2,1)S(1)}, bf16[2,256,512]{1,2,0:T(8,128)(2,1)}, u32[]{:S(2)}, u32[]{:S(2)}) collective-permute-start(bf16[2,256,512]{1,2,0:T(8,128)(2,1)S(1)} %pad_maximum_fusion.1), channel_id=1, source_target_pairs={{2,0},{4,2},{6,4},{8,6},{10,8},{12,10},{14,12},{16,14},{18,16},{20... | collective-permute-start | bytes 1572872 | tf_op jit(solution)/shard_map/ppermute | solution.py:28
  3.6 14.7 %collective-permute-start = (bf16[2,256,512]{1,2,0:T(8,128)(2,1)S(1)}, bf16[2,256,512]{1,2,0:T(8,128)(2,1)}, u32[]{:S(2)}, u32[]{:S(2)}) collective-permute-start(bf16[2,256,512]{1,2,0:T(8,128)(2,1)S(1)} %pad_maximum_fusion.1), channel_id=1, source_target_pairs={{0,2},{2,4},{4,6},{6,8},{8,10},{10,12},{12,14},{14,16},{16,18},{18... | collective-permute-start | bytes 1572872 | tf_op jit(solution)/shard_map/ppermute | solution.py:26
  9.0 16.5 %collective-permute-start.3 = (bf16[512,2048]{1,0:T(8,128)(2,1)}, bf16[512,2048]{1,0:T(8,128)(2,1)S(1)}, u32[]{:S(2)}, u32[]{:S(2)}) collective-permute-start(bf16[512,2048]{1,0:T(8,128)(2,1)} %param.17), channel_id=1, source_target_pairs={{0,1},{1,0},{2,3},{3,2},{4,5},{5,4},{6,7},{7,6},{8,9},{9,8},{10,11... | collective-permute-start | bytes 6291464 | tf_op jit(solution)/shard_map/ppermute | solution.py:35
  21.9 2.6 %copy-start.2 = (bf16[512,2048]{1,0:T(8,128)(2,1)S(1)}, bf16[512,2048]{1,0:T(8,128)(2,1)}, u32[]{:S(2)}) copy-start(bf16[512,2048]{1,0:T(8,128)(2,1)} %param.17) | copy-start | bytes 6291460
  21.9 2.6 %copy-start.3 = (bf16[128,2048]{1,0:T(8,128)(2,1)S(1)}, bf16[128,2048]{1,0:T(8,128)(2,1)}, u32[]{:S(2)}) copy-start(bf16[128,2048]{1,0:T(8,128)(2,1)} %param.15) | copy-start | bytes 1572868
  22.4 3.7 %copy-start.4 = (f32[2048]{0:T(1024)S(1)}, f32[2048]{0:T(1024)}, u32[]{:S(2)}) copy-start(f32[2048]{0:T(1024)} %param.18) | copy-start | bytes 24580
  22.4 3.1 %collective-permute-start.2 = (bf16[128,512]{0,1:T(8,128)(2,1)S(1)}, bf16[128,512]{0,1:T(8,128)(2,1)S(1)}, u32[]{:S(2)}, u32[]{:S(2)}) collective-permute-start(bf16[128,512]{0,1:T(8,128)(2,1)S(1)} %constant_dynamic-slice_fusion), channel_id=1, source_target_pairs={{0,1},{1,0},{2,3},{3,2},{4,5},{5,4},{6,7},{7,6},{8,9},{9,8},{10,11... | collective-permute-start | bytes 393224 | tf_op jit(solution)/shard_map/ppermute | solution.py:35
  26.0 1.2 copy-start.1
